TPU v7x, 32 devices: a whole 2x2x4 slice. The times are simulated.
32 devices in a mesh: snap: 8 (over z, x), feat: 4 (over y, core).
Axes of the slice: x: 2, y: 2, z: 4, core: 2. Of those that a mesh axis runs over, the one named last changes fastest.
Arguments:
- node_features: bfloat16 [16, 512, 256], P('snap', None, 'feat'), may hold values from -6 to 6
- tile_rows: int32 [16, 8], P('snap'), may hold values from 0 to 3
- tile_cols: int32 [16, 8], P('snap'), may hold values from 0 to 3, as said below
- tile_counts: int32 [16], P('snap'), may hold values from 4 to 8, as said below
- tile_values: bfloat16 [16, 8, 128, 128], P('snap'), may hold values from -0.5 to 0.5
- layer_one: bfloat16 [256, 256], replicated, may hold values from -0.375 to 0.375
- layer_two: bfloat16 [256, 256], replicated, may hold values from -0.375 to 0.375
- query_weight: bfloat16 [256, 256], replicated, may hold values from -1.25 to 1.25
- key_weight: bfloat16 [256, 256], replicated, may hold values from -1.25 to 1.25
- value_weight: bfloat16 [256, 256], replicated, may hold values from -0.375 to 0.375
- out_weight: bfloat16 [256, 256], replicated, may hold values from -0.375 to 0.375
Outputs:
- evolved: bfloat16 [16, 512, 256], P('snap', None, 'feat')
Inputs may be any that keep to these rules, and one draw needn't show every extreme that they name: `tile_cols`: block columns of the tile slots; a coordinate pair may be listed more than once, and such tiles add. `tile_counts`: some snapshot uses all 8 slots.
All inputs are finite; a program needn't handle non-finite values.
Results may differ from a plain program's by a relative error of at most 0.02.
The roundings to bfloat16 on the way count: a program that leaves them out, or rounds other values in their place, can miss the bound.
Values may be sent and summed in bfloat16 or wider, within the bound.
A program may use at most 64 MiB of HBM per device.

v0:
```python
import functools
import math

import jax
import jax.numpy as jnp
from jax import lax
from jax.experimental import pallas as pl
from jax.experimental.pallas import tpu as pltpu
from jax.sharding import PartitionSpec as P

HEADS = 8


masked_score = -1e30


def spread_padded(features, tile_block, block_rows, block_cols, slot_count):
    vert_count, feat_width = features.shape
    tile_side = tile_block.shape[1]
    slot_total = tile_block.shape[0]
    block_count = vert_count // tile_side
    blocked = features.reshape(block_count, tile_side, feat_width)
    picked_blocks = blocked[block_cols]
    live_slots = jnp.arange(slot_total, dtype=jnp.int32) < slot_count
    products = jnp.einsum(
        "irc,icf->irf", tile_block, picked_blocks, preferred_element_type=jnp.float32
    )
    products = products * live_slots.astype(jnp.float32)[:, None, None]
    membership = (
        (block_rows[None, :] == jnp.arange(block_count, dtype=jnp.int32)[:, None])
        & live_slots[None, :]
    ).astype(jnp.float32)
    summed = jnp.dot(
        membership,
        products.reshape(slot_total, tile_side * feat_width),
        precision=lax.Precision.HIGHEST,
    )
    return summed.reshape(vert_count, feat_width).astype(jnp.bfloat16)


def attend_local(hidden, query_weight, key_weight, value_weight, out_weight):
    snaps, verts, model_width = hidden.shape
    head_dim = model_width // HEADS
    flat = hidden.reshape(snaps * verts, model_width)

    def project(weight):
        return (
            jnp.dot(flat, weight, preferred_element_type=jnp.float32)
            .astype(jnp.bfloat16)
            .reshape(snaps, verts, HEADS, head_dim)
        )

    query_heads = project(query_weight)
    key_heads = project(key_weight)
    value_heads = project(value_weight)
    scores = jnp.einsum(
        "tvhd,uvhd->vhtu", query_heads, key_heads, preferred_element_type=jnp.float32
    ) * head_dim ** (-0.5)
    causal = (
        jnp.arange(snaps, dtype=jnp.int32)[:, None] >= jnp.arange(snaps, dtype=jnp.int32)[None, :]
    )
    scores = jnp.where(causal, scores, masked_score)
    row_max = jnp.max(scores, axis=-1, keepdims=True)
    lifted = jnp.exp(scores - row_max)
    weights = (lifted / jnp.sum(lifted, axis=-1, keepdims=True)).astype(jnp.bfloat16)
    context = jnp.einsum(
        "vhtu,uvhd->tvhd", weights, value_heads, preferred_element_type=jnp.float32
    ).astype(jnp.bfloat16)
    context = context.reshape(snaps * verts, model_width)
    result = flat.astype(jnp.float32) + jnp.dot(
        context, out_weight, preferred_element_type=jnp.float32
    )
    return result.astype(jnp.bfloat16).reshape(snaps, verts, model_width)


def on_device(
    node_features,
    tile_rows,
    tile_cols,
    tile_counts,
    tile_values,
    layer_one,
    layer_two,
    query_weight,
    key_weight,
    value_weight,
    out_weight,
):
    snap_dev, vert_count, feat_width = node_features.shape
    feat_index = lax.axis_index("feat")

    def spread_all(features):
        spread_pieces = []
        for snapshot in range(snap_dev):
            spread_pieces.append(
                spread_padded(
                    features[snapshot],
                    tile_values[snapshot],
                    tile_rows[snapshot],
                    tile_cols[snapshot],
                    tile_counts[snapshot],
                )
            )
        return jnp.stack(spread_pieces, axis=0)

    def convolve(features, weight):
        spread_rows = spread_all(features).reshape(snap_dev * vert_count, feat_width)
        own_columns = lax.dynamic_slice_in_dim(weight, feat_index * feat_width, feat_width, 1)
        mixed_sum = jnp.dot(
            lax.all_gather(spread_rows, "feat", axis=1, tiled=True),
            own_columns,
            preferred_element_type=jnp.float32,
        )
        mixed_sum = mixed_sum.reshape(snap_dev, vert_count, feat_width)
        return (features.astype(jnp.float32) + jnp.maximum(mixed_sum, 0.0)).astype(jnp.bfloat16)

    hidden_one = convolve(node_features, layer_one)
    hidden_two = convolve(hidden_one, layer_two)
    vertex_rows = lax.all_to_all(
        lax.all_to_all(hidden_two, "snap", split_axis=1, concat_axis=0, tiled=True),
        "feat",
        split_axis=1,
        concat_axis=2,
        tiled=True,
    )
    attended = attend_local(vertex_rows, query_weight, key_weight, value_weight, out_weight)
    return lax.all_to_all(
        lax.all_to_all(attended, "feat", split_axis=2, concat_axis=1, tiled=True),
        "snap",
        split_axis=0,
        concat_axis=1,
        tiled=True,
    )


LANES = 128
SUBLANES = 8
MESH = pl.DeviceIdType.MESH


def fused_kernel(
    n_snap,
    n_feat,
    rows_hbm,
    cols_hbm,
    counts_hbm,
    feat_ref,
    tiles_ref,
    w_one,
    w_two,
    w_query,
    w_key,
    w_value,
    w_out,
    returned,
    tiles,
    weights,
    pieces,
    adjacency,
    features,
    hidden_one,
    hidden_two,
    vertex_rows,
    outgoing,
    load_sem,
    gather_send,
    gather_recv,
    spread_send,
    spread_recv,
    return_send,
    return_recv,
    heard,
    rows_ref,
    cols_ref,
    counts_ref,
):
    snap_dev, feat_width, vert_count = feat_ref.shape
    slot_total, tile_side, _ = tiles.shape
    block_count = vert_count // tile_side
    snaps, vert_dev, width = vertex_rows.shape
    parts = n_feat // snap_dev
    part_rows = vert_count // parts
    total = n_snap * n_feat
    head_dim = width // HEADS

    me_snap = lax.axis_index("snap")
    me_feat = lax.axis_index("feat")
    me = me_snap * n_feat + me_feat
    part = me_feat % parts
    local = me_feat // parts
    own = me_snap * snap_dev + local

    def load(source, target, at):
        copy = pltpu.make_async_copy(source, target, load_sem.at[at])
        copy.start()
        return copy

    barrier = pltpu.get_barrier_semaphore()
    twin = me_snap + 1 - 2 * (me_snap % 2)
    ring = [(me_snap + 2) % n_snap, (me_snap + n_snap - 2) % n_snap]
    mates = [(me_feat + step) % n_feat for step in range(1, n_feat)]

    def tell(semaphore, peers):
        for peer in peers:
            pl.semaphore_signal(semaphore, inc=1, device_id=peer, device_id_type=MESH)

    ring_peers = [(peer, me_feat) for peer in ring]
    twin_peer = [(twin, me_feat)]
    mate_peers = [(me_snap, mate) for mate in mates]
    tell(barrier, ring_peers + twin_peer + mate_peers)
    list_loads = [
        load(ref, kept, 8 + at)
        for at, (ref, kept) in enumerate(
            ((rows_hbm, rows_ref), (cols_hbm, cols_ref), (counts_hbm, counts_ref))
        )
    ]
    tile_load = load(tiles_ref.at[local], tiles, 1)
    pl.semaphore_wait(barrier, len(ring_peers) + 1 + len(mate_peers))

    gathers = []
    for step in [n_feat // 2] + [s for s in range(1, n_feat) if s != n_feat // 2]:
        peer = (me_feat + step) % n_feat
        copy = pltpu.make_async_remote_copy(
            src_ref=feat_ref.at[peer // parts],
            dst_ref=pieces.at[me_feat],
            send_sem=gather_send.at[step],
            recv_sem=gather_recv.at[step],
            device_id=(me_snap, peer),
            device_id_type=MESH,
        )
        copy.start()
        gathers.append(copy)
    weight_loads = [
        load(ref, weights.at[at], 2 + at)
        for at, ref in enumerate((w_one, w_two, w_query, w_key, w_value, w_out))
    ]
    own_load = load(feat_ref.at[local], pieces.at[me_feat], 0)

    hops = n_snap // 4 - 1
    for hop in range(hops):
        tell(heard.at[hop], ring_peers)
        if hop + 1 < hops:
            pl.semaphore_wait(heard.at[hop], len(ring_peers))

    tile_load.wait()
    for copy in list_loads:
        copy.wait()
    slot_count = counts_ref[local]
    strip = 2 * SUBLANES
    places = []
    for slot in range(slot_total):
        place = rows_ref[local, slot] * block_count + cols_ref[local, slot]
        place = jnp.where(slot < slot_count, place, -1)
        places.append(jnp.full((strip, tile_side), place, jnp.int32))

    def build(at, carry):
        first = pl.multiple_of(at * strip, strip)
        listed = [
            tiles[slot, pl.ds(first, strip), :].astype(jnp.float32) for slot in range(slot_total)
        ]
        for row in range(block_count):
            for col in range(block_count):
                summed = jnp.zeros((strip, tile_side), jnp.float32)
                for slot in range(slot_total):
                    summed += jnp.where(
                        places[slot] == row * block_count + col, listed[slot], 0.0
                    )
                start = pl.multiple_of(row * tile_side + first, strip)
                adjacency[pl.ds(start, strip), col * tile_side : (col + 1) * tile_side] = (
                    summed.astype(jnp.bfloat16)
                )
        return carry

    strips = tile_side // strip
    lax.fori_loop(0, strips // 2, build, 0)
    pl.semaphore_wait(heard.at[hops - 1], len(ring_peers))
    tell(heard.at[hops], twin_peer)
    lax.fori_loop(strips // 2, strips, build, 0)
    pl.semaphore_wait(heard.at[hops], 1)
    tell(heard.at[hops + 1], mate_peers)

    for copy in weight_loads:
        copy.wait()
    for copy in gathers:
        copy.wait_recv()
    own_load.wait()
    features[...] = jnp.transpose(pieces[...].reshape(width, vert_count))

    def mix(lhs, source, before, weight):
        spread = jnp.dot(lhs, source, preferred_element_type=jnp.float32)
        mixed = jnp.dot(
            spread.astype(jnp.bfloat16), weight, preferred_element_type=jnp.float32
        )
        return (before.astype(jnp.float32) + jnp.maximum(mixed, 0.0)).astype(jnp.bfloat16)

    hidden_one[...] = mix(adjacency[...], features[...], features[...], weights[0])
    pl.semaphore_wait(heard.at[hops + 1], len(mate_peers))
    side = snaps // 2
    side_rows = side * vert_dev
    sends = []
    for turn in range(2):
        first = (own // side + 1 - turn) % 2 * side
        start = pl.multiple_of(part * part_rows + first * vert_dev, side_rows)
        own_rows = pl.ds(start, side_rows)
        hidden_two[pl.ds(first, side)] = mix(
            adjacency[own_rows, :], hidden_one[...], hidden_one[own_rows, :], weights[1]
        ).reshape(side, vert_dev, width)
        for step in range(turn, side):
            peer = first + (own % side + step) % side
            at = step + (1 - turn) * side
            copy = pltpu.make_async_remote_copy(
                src_ref=hidden_two.at[peer],
                dst_ref=vertex_rows.at[own],
                send_sem=spread_send.at[at],
                recv_sem=spread_recv.at[(own - peer + snaps) % snaps],
                device_id=(peer // snap_dev, (peer % snap_dev) * parts + part),
                device_id_type=MESH,
            )
            copy.start()
            sends.append(copy)
    vertex_rows[own] = hidden_two[own]
    for source in range(1, snaps):
        pltpu.make_async_copy(
            hidden_two.at[0], vertex_rows.at[0], spread_recv.at[source]
        ).wait()

    flat = vertex_rows[...].reshape(snaps * vert_dev, width)
    group_rows = snaps * SUBLANES
    groups = vert_dev // SUBLANES

    def split(array):
        array = array.reshape(snaps, groups, SUBLANES, width)
        return [array[:, at].reshape(group_rows, width) for at in range(groups)]

    def project(at):
        return split(jnp.dot(flat, weights[at], preferred_element_type=jnp.float32))

    queries, keys, values = project(2), project(3), project(4)
    before = split(flat.astype(jnp.float32))
    lane_head = lax.broadcasted_iota(jnp.int32, (group_rows, width), 1) // head_dim
    row_at = lax.broadcasted_iota(jnp.int32, (group_rows, group_rows), 0)
    col_at = lax.broadcasted_iota(jnp.int32, (group_rows, group_rows), 1)
    visible = (row_at % SUBLANES == col_at % SUBLANES) & (
        row_at // SUBLANES <= col_at // SUBLANES
    )
    factor = head_dim ** (-0.5) * math.log2(math.e)
    results = []
    for at in range(groups):
        query = queries[at].astype(jnp.bfloat16)
        value = jnp.transpose(values[at].astype(jnp.bfloat16))
        key = jnp.concatenate(
            [
                jnp.where(lane_head == head, keys[at], 0.0).astype(jnp.bfloat16)
                for head in range(HEADS)
            ],
            axis=0,
        )
        scores = lax.dot_general(
            key, query, (((1,), (1,)), ((), ())), preferred_element_type=jnp.float32
        )
        context = []
        for head in range(HEADS):
            score = scores[head * group_rows : (head + 1) * group_rows]
            score = jnp.where(visible, score, masked_score)
            lifted = jnp.exp2((score - jnp.max(score, axis=0, keepdims=True)) * factor)
            scale = 1.0 / jnp.sum(lifted, axis=0, keepdims=True)
            context.append(
                jnp.dot(
                    value[head * head_dim : (head + 1) * head_dim],
                    (lifted * scale).astype(jnp.bfloat16),
                    preferred_element_type=jnp.float32,
                )
            )
        context = jnp.transpose(jnp.concatenate(context, axis=0).astype(jnp.bfloat16))
        result = before[at] + jnp.dot(context, weights[5], preferred_element_type=jnp.float32)
        results.append(result.reshape(snaps, 1, SUBLANES, width))
    evolved = jnp.concatenate(results, axis=1).reshape(n_snap, snap_dev, vert_dev, width)

    low = lax.broadcasted_iota(jnp.int32, (n_snap * vert_dev, LANES), 1) < feat_width
    for at in range(0, n_feat, 2):
        lanes = slice(at * feat_width, (at + 2) * feat_width)
        first = evolved[:, 0, :, lanes].reshape(n_snap * vert_dev, LANES)
        second = evolved[:, 1, :, lanes].reshape(n_snap * vert_dev, LANES)
        even = jnp.where(low, first, pltpu.roll(second, feat_width, 1))
        odd = jnp.where(low, pltpu.roll(first, feat_width, 1), second)
        outgoing[at] = even.astype(jnp.bfloat16).reshape(n_snap, vert_dev, LANES)
        outgoing[at + 1] = odd.astype(jnp.bfloat16).reshape(n_snap, vert_dev, LANES)

    returns = []
    for step in sorted(range(1, total), key=lambda s: abs(2 * s - total)):
        peer = (me + step) % total
        copy = pltpu.make_async_remote_copy(
            src_ref=outgoing.at[peer % n_feat, peer // n_feat],
            dst_ref=returned.at[part, own],
            send_sem=return_send.at[step],
            recv_sem=return_recv.at[step],
            device_id=(peer // n_feat, peer % n_feat),
            device_id_type=MESH,
        )
        copy.start()
        returns.append(copy)
    own_copy = load(outgoing.at[me_feat, me_snap], returned.at[part, own], 0)
    for copy in gathers + sends:
        copy.wait_send()
    own_copy.wait()
    for copy in returns:
        copy.wait_recv()
    for copy in returns:
        copy.wait_send()


def on_device_fused(n_snap, n_feat, *operands):
    node_features, _, _, _, tile_values, layer_one = operands[:6]
    snap_dev, vert_count, feat_width = node_features.shape
    _, slot_total, tile_side, _ = tile_values.shape
    width = layer_one.shape[0]
    parts = n_feat // snap_dev
    snaps = n_snap * snap_dev
    vert_dev = vert_count // (parts * snaps)
    total = n_snap * n_feat
    kept = jnp.bfloat16
    result = pl.pallas_call(
        functools.partial(fused_kernel, n_snap, n_feat),
        out_shape=jax.ShapeDtypeStruct((parts, snaps, vert_dev, LANES), kept),
        in_specs=[pl.BlockSpec(memory_space=pltpu.HBM)] * 11,
        out_specs=pl.BlockSpec(memory_space=pl.ANY),
        scratch_shapes=[
            pltpu.VMEM((slot_total, tile_side, tile_side), kept),
            pltpu.VMEM((6, width, width), kept),
            pltpu.VMEM((n_feat, feat_width, vert_count), kept),
            pltpu.VMEM((vert_count, vert_count), kept),
            pltpu.VMEM((vert_count, width), kept),
            pltpu.VMEM((vert_count, width), kept),
            pltpu.VMEM((snaps, vert_dev, width), kept),
            pltpu.VMEM((snaps, vert_dev, width), kept),
            pltpu.VMEM((n_feat, n_snap, vert_dev, LANES), kept),
            pltpu.SemaphoreType.DMA((11,)),
            pltpu.SemaphoreType.DMA((n_feat,)),
            pltpu.SemaphoreType.DMA((n_feat,)),
            pltpu.SemaphoreType.DMA((snaps,)),
            pltpu.SemaphoreType.DMA((snaps,)),
            pltpu.SemaphoreType.DMA((total,)),
            pltpu.SemaphoreType.DMA((total,)),
            pltpu.SemaphoreType.REGULAR((n_snap // 4 + 1,)),
            pltpu.SMEM((snap_dev, slot_total), jnp.int32),
            pltpu.SMEM((snap_dev, slot_total), jnp.int32),
            pltpu.SMEM((snap_dev,), jnp.int32),
        ],
        compiler_params=pltpu.CompilerParams(collective_id=0, has_side_effects=True),
    )(*operands[1:4], node_features.transpose(0, 2, 1), *operands[4:])
    result = jnp.transpose(result.reshape(vert_count, LANES))
    return result.reshape(snap_dev, feat_width, vert_count).transpose(0, 2, 1)


def dispatch(n_snap, n_feat, *operands):
    snap_dev, vert_count, feat_width = operands[0].shape
    slot_total = operands[4].shape[1]
    snaps = n_snap * snap_dev
    fits = (
        snap_dev == 2
        and 2 * feat_width == LANES
        and n_feat % snap_dev == 0
        and n_feat % 2 == 0
        and n_snap >= 8
        and n_snap % 4 == 0
        and vert_count % (n_feat // snap_dev * snaps * 2 * SUBLANES) == 0
        and snaps * SUBLANES == LANES
        and slot_total <= 16
        and vert_count <= 1024
    )
    if fits:
        return on_device_fused(n_snap, n_feat, *operands)
    return on_device(*operands)


def solution(mesh):
    placed = (
        P("snap", None, "feat"),
        P("snap", None),
        P("snap", None),
        P("snap"),
        P("snap", None, None, None),
        P(),
        P(),
        P(),
        P(),
        P(),
        P(),
    )
    return jax.shard_map(
        functools.partial(dispatch, mesh.shape["snap"], mesh.shape["feat"]), mesh=mesh, in_specs=placed, out_specs=P("snap", None, "feat"), check_vma=False
    )
```

profile of v0, /device:TPU:0, one launch (start us, length us, event | category | flops | bytes accessed | tf_op | source)
XLA Modules:
  0.0 26.0 jit_solution(16790294127759188737)
XLA Ops:
  0.0 24.3 %shard_map.109 = bf16[2,16,16,128]{3,2,1,0:T(8,128)(2,1)} custom-call(s32[2,8]{1,0:T(2,128)} %rows_hbm.1, s32[2,8]{1,0:T(2,128)} %cols_hbm.1, s32[2]{0:T(128)} %counts_hbm.1, bf16[2,64,512]{2,1,0:T(8,128)(2,1)} %bitcast.8, bf16[2,8,128,128]{3,2,1,0:T(8,128)(2,1)} %tiles_ref.1, bf16[256,256]{1,0:T(8,128)(2,1)} %w_one.1, bf16[256,256]{1,0:T(8,128)(2,1)} %w_two.1, ...), custom_call_target="tpu_custom_call" | custom-call | tf_op jit(solution)/shard_map/pallas_call | solution.py:422
  24.3 1.7 %copy.12 = bf16[128,512]{1,0:T(8,128)(2,1)} copy(bf16[128,512]{0,1:T(8,128)(2,1)} %bitcast.7) | data formatting | bytes 262144 | tf_op jit(solution)/shard_map/transpose | solution.py:451
where the time goes:
time: 26.1 us; the launch traced here: 26 us
  Pallas kernels  24.3 us (93%)
  local copies, waits for them, and re-layouts  1.67 us (6%)
    pallas_call x1, Pallas kernels, on_device_fused(): pl.pallas_call(functools.partial(fused_kernel, n_snap, n_feat), out_shape...  24.3 us
    transpose x1, local copies, waits for them, and re-layouts, on_device_fused(): result = jnp.transpose(result.reshape(vert_count, LANES))  1.67 us

commit v1 on v0

--- a/solution.py
+++ b/solution.py
@@ -178,69 +178,84 @@
     slot_total, tile_side, _ = tiles.shape
     block_count = vert_count // tile_side
     snaps, vert_dev, width = vertex_rows.shape
+    half_snaps = snaps // 2
     parts = n_feat // snap_dev
     part_rows = vert_count // parts
-    total = n_snap * n_feat
     head_dim = width // HEADS
 
     me_snap = lax.axis_index("snap")
     me_feat = lax.axis_index("feat")
-    me = me_snap * n_feat + me_feat
     part = me_feat % parts
     local = me_feat // parts
     own = me_snap * snap_dev + local
+    half = own // half_snaps
+    rank = own % half_snaps
+    is_low = half == 0
+    is_high = half == 1
 
     def load(source, target, at):
         copy = pltpu.make_async_copy(source, target, load_sem.at[at])
         copy.start()
         return copy
 
+    def settle(ref, semaphore):
+        pltpu.make_async_copy(ref, ref, semaphore).wait()
+
     barrier = pltpu.get_barrier_semaphore()
+    plane = 2
     twin = me_snap + 1 - 2 * (me_snap % 2)
-    ring = [(me_snap + 2) % n_snap, (me_snap + n_snap - 2) % n_snap]
     mates = [(me_feat + step) % n_feat for step in range(1, n_feat)]
-
-    def tell(semaphore, peers):
-        for peer in peers:
-            pl.semaphore_signal(semaphore, inc=1, device_id=peer, device_id_type=MESH)
-
-    ring_peers = [(peer, me_feat) for peer in ring]
-    twin_peer = [(twin, me_feat)]
-    mate_peers = [(me_snap, mate) for mate in mates]
-    tell(barrier, ring_peers + twin_peer + mate_peers)
+    has_below = me_snap >= plane
+    has_above = me_snap < n_snap - plane
+    column_count = has_below.astype(jnp.int32) + has_above.astype(jnp.int32)
+
+    def signal(semaphore, peer):
+        pl.semaphore_signal(semaphore, inc=1, device_id=peer, device_id_type=MESH)
+
+    def tell_column(semaphore):
+        @pl.when(has_below)
+        def _():
+            signal(semaphore, (me_snap - plane, me_feat))
+
+        @pl.when(has_above)
+        def _():
+            signal(semaphore, (me_snap + plane, me_feat))
+
+    def tell_mates(semaphore):
+        for mate in mates:
+            signal(semaphore, (me_snap, mate))
+
+    tell_mates(barrier)
+    signal(barrier, (twin, me_feat))
+    tell_column(barrier)
     list_loads = [
-        load(ref, kept, 8 + at)
+        load(ref, kept, 2 + at)
         for at, (ref, kept) in enumerate(
             ((rows_hbm, rows_ref), (cols_hbm, cols_ref), (counts_hbm, counts_ref))
         )
     ]
     tile_load = load(tiles_ref.at[local], tiles, 1)
-    pl.semaphore_wait(barrier, len(ring_peers) + 1 + len(mate_peers))
-
-    gathers = []
+    pl.semaphore_wait(barrier, n_feat + column_count)
+
     for step in [n_feat // 2] + [s for s in range(1, n_feat) if s != n_feat // 2]:
         peer = (me_feat + step) % n_feat
-        copy = pltpu.make_async_remote_copy(
+        pltpu.make_async_remote_copy(
             src_ref=feat_ref.at[peer // parts],
             dst_ref=pieces.at[me_feat],
-            send_sem=gather_send.at[step],
-            recv_sem=gather_recv.at[step],
+            send_sem=gather_send,
+            recv_sem=gather_recv,
             device_id=(me_snap, peer),
             device_id_type=MESH,
-        )
-        copy.start()
-        gathers.append(copy)
-    weight_loads = [
-        load(ref, weights.at[at], 2 + at)
-        for at, ref in enumerate((w_one, w_two, w_query, w_key, w_value, w_out))
-    ]
+        ).start()
+    for at, ref in enumerate((w_one, w_two, w_query, w_key, w_value, w_out)):
+        load(ref, weights.at[at], 5)
     own_load = load(feat_ref.at[local], pieces.at[me_feat], 0)
 
-    hops = n_snap // 4 - 1
+    hops = n_snap // plane - 2
     for hop in range(hops):
-        tell(heard.at[hop], ring_peers)
+        tell_column(heard.at[hop])
         if hop + 1 < hops:
-            pl.semaphore_wait(heard.at[hop], len(ring_peers))
+            pl.semaphore_wait(heard.at[hop], column_count)
 
     tile_load.wait()
     for copy in list_loads:
@@ -273,16 +288,14 @@
 
     strips = tile_side // strip
     lax.fori_loop(0, strips // 2, build, 0)
-    pl.semaphore_wait(heard.at[hops - 1], len(ring_peers))
-    tell(heard.at[hops], twin_peer)
+    pl.semaphore_wait(heard.at[hops - 1], column_count)
+    signal(heard.at[hops], (twin, me_feat))
     lax.fori_loop(strips // 2, strips, build, 0)
     pl.semaphore_wait(heard.at[hops], 1)
-    tell(heard.at[hops + 1], mate_peers)
-
-    for copy in weight_loads:
-        copy.wait()
-    for copy in gathers:
-        copy.wait_recv()
+    tell_mates(heard.at[hops + 1])
+
+    settle(weights, load_sem.at[5])
+    settle(pieces.at[pl.ds(0, n_feat - 1)], gather_recv)
     own_load.wait()
     features[...] = jnp.transpose(pieces[...].reshape(width, vert_count))
 
@@ -294,119 +307,178 @@
         return (before.astype(jnp.float32) + jnp.maximum(mixed, 0.0)).astype(jnp.bfloat16)
 
     hidden_one[...] = mix(adjacency[...], features[...], features[...], weights[0])
-    pl.semaphore_wait(heard.at[hops + 1], len(mate_peers))
-    side = snaps // 2
-    side_rows = side * vert_dev
-    sends = []
-    for turn in range(2):
-        first = (own // side + 1 - turn) % 2 * side
-        start = pl.multiple_of(part * part_rows + first * vert_dev, side_rows)
-        own_rows = pl.ds(start, side_rows)
-        hidden_two[pl.ds(first, side)] = mix(
-            adjacency[own_rows, :], hidden_one[...], hidden_one[own_rows, :], weights[1]
-        ).reshape(side, vert_dev, width)
-        for step in range(turn, side):
-            peer = first + (own % side + step) % side
-            at = step + (1 - turn) * side
-            copy = pltpu.make_async_remote_copy(
-                src_ref=hidden_two.at[peer],
-                dst_ref=vertex_rows.at[own],
-                send_sem=spread_send.at[at],
-                recv_sem=spread_recv.at[(own - peer + snaps) % snaps],
-                device_id=(peer // snap_dev, (peer % snap_dev) * parts + part),
-                device_id_type=MESH,
-            )
-            copy.start()
-            sends.append(copy)
-    vertex_rows[own] = hidden_two[own]
-    for source in range(1, snaps):
-        pltpu.make_async_copy(
-            hidden_two.at[0], vertex_rows.at[0], spread_recv.at[source]
-        ).wait()
-
-    flat = vertex_rows[...].reshape(snaps * vert_dev, width)
-    group_rows = snaps * SUBLANES
+    pl.semaphore_wait(heard.at[hops + 1], len(mates))
+
+    def spread_to(target_half, peer):
+        target = target_half * half_snaps + peer
+        pltpu.make_async_remote_copy(
+            src_ref=hidden_two.at[peer],
+            dst_ref=vertex_rows.at[own],
+            send_sem=spread_send.at[target_half],
+            recv_sem=spread_recv.at[half],
+            device_id=(target // snap_dev, (target % snap_dev) * parts + part),
+            device_id_type=MESH,
+        ).start()
+
+    def spread_half(target_half):
+        for step in [half_snaps // 2] + [
+            s for s in range(1, half_snaps) if s != half_snaps // 2
+        ]:
+            spread_to(target_half, (rank + step) % half_snaps)
+
+    own_rows = pl.ds(pl.multiple_of(part * part_rows, part_rows), part_rows)
+    hidden_two[...] = mix(
+        adjacency[own_rows, :], hidden_one[...], hidden_one[own_rows, :], weights[1]
+    ).reshape(half_snaps, vert_dev, width)
+    side = half_snaps // 2
+    far = [side + (rank + step) % side for step in range(side)]
+    near = [(rank + step) % side for step in range(side)]
+
+    @pl.when(is_low)
+    def _():
+        spread_half(0)
+        for peer in far + near:
+            spread_to(1, peer)
+
+    @pl.when(is_high)
+    def _():
+        spread_half(1)
+
+    vertex_rows[own] = hidden_two[rank]
+
     groups = vert_dev // SUBLANES
+    group_rows = half_snaps * SUBLANES
+    columns = HEADS * group_rows
 
     def split(array):
-        array = array.reshape(snaps, groups, SUBLANES, width)
+        array = array.reshape(half_snaps, groups, SUBLANES, width)
         return [array[:, at].reshape(group_rows, width) for at in range(groups)]
 
-    def project(at):
+    def project(flat, at):
         return split(jnp.dot(flat, weights[at], preferred_element_type=jnp.float32))
 
-    queries, keys, values = project(2), project(3), project(4)
+    def score(keys, queries):
+        return lax.dot_general(
+            keys.astype(jnp.bfloat16),
+            queries,
+            (((1,), (1,)), ((), ())),
+            preferred_element_type=jnp.float32,
+        )
+
+    row_at = lax.broadcasted_iota(jnp.int32, (group_rows, columns), 0)
+    col_at = lax.broadcasted_iota(jnp.int32, (group_rows, columns), 1) % group_rows
+    same = row_at % SUBLANES == col_at % SUBLANES
+    visible = same & (row_at // SUBLANES <= col_at // SUBLANES)
+    visible_low = same & (jnp.full((group_rows, columns), half, jnp.int32) == 1)
+    lane_head = lax.broadcasted_iota(jnp.int32, (group_rows, width), 1) // head_dim
+    factor = head_dim ** (-0.5) * math.log2(math.e)
+
+    settle(vertex_rows.at[pl.ds(0, half_snaps - 1)], spread_recv.at[half])
+    own_rows = vertex_rows[pl.ds(half * half_snaps, half_snaps)]
+    flat = own_rows.reshape(half_snaps * vert_dev, width)
     before = split(flat.astype(jnp.float32))
-    lane_head = lax.broadcasted_iota(jnp.int32, (group_rows, width), 1) // head_dim
-    row_at = lax.broadcasted_iota(jnp.int32, (group_rows, group_rows), 0)
-    col_at = lax.broadcasted_iota(jnp.int32, (group_rows, group_rows), 1)
-    visible = (row_at % SUBLANES == col_at % SUBLANES) & (
-        row_at // SUBLANES <= col_at // SUBLANES
-    )
-    factor = head_dim ** (-0.5) * math.log2(math.e)
-    results = []
-    for at in range(groups):
-        query = queries[at].astype(jnp.bfloat16)
-        value = jnp.transpose(values[at].astype(jnp.bfloat16))
-        key = jnp.concatenate(
+    queries = [
+        jnp.concatenate(
             [
-                jnp.where(lane_head == head, keys[at], 0.0).astype(jnp.bfloat16)
+                jnp.where(lane_head == head, query, 0.0).astype(jnp.bfloat16)
                 for head in range(HEADS)
             ],
             axis=0,
         )
-        scores = lax.dot_general(
-            key, query, (((1,), (1,)), ((), ())), preferred_element_type=jnp.float32
+        for query in project(flat, 2)
+    ]
+    keys, values = project(flat, 3), project(flat, 4)
+    scores = [
+        jnp.where(visible, score(keys[at], queries[at]), masked_score)
+        for at in range(groups)
+    ]
+
+    @pl.when(is_high)
+    def _():
+        settle(vertex_rows.at[pl.ds(0, half_snaps)], spread_recv.at[0])
+
+    flat_low = vertex_rows[pl.ds(0, half_snaps)].reshape(half_snaps * vert_dev, width)
+    keys_low, values_low = project(flat_low, 3), project(flat_low, 4)
+    pair = 2 * group_rows
+    pair_dims = 2 * head_dim
+    pair_row = lax.broadcasted_iota(jnp.int32, (pair_dims, pair), 0) // head_dim
+    pair_col = lax.broadcasted_iota(jnp.int32, (pair_dims, pair), 1) // group_rows
+    contexts = []
+    for at in range(groups):
+        score_low = jnp.where(visible_low, score(keys_low[at], queries[at]), masked_score)
+        score_own = scores[at]
+        highest = jnp.maximum(
+            jnp.max(score_low, axis=0, keepdims=True), jnp.max(score_own, axis=0, keepdims=True)
+        )
+        lifted_low = jnp.exp2((score_low - highest) * factor)
+        lifted_own = jnp.exp2((score_own - highest) * factor)
+        scale = 1.0 / (
+            jnp.sum(lifted_low, axis=0, keepdims=True) + jnp.sum(lifted_own, axis=0, keepdims=True)
+        )
+        shares = jnp.concatenate(
+            [(lifted_low * scale).astype(jnp.bfloat16), (lifted_own * scale).astype(jnp.bfloat16)],
+            axis=0,
+        )
+        value = jnp.transpose(
+            jnp.concatenate([values_low[at], values[at]], axis=0).astype(jnp.bfloat16)
         )
         context = []
-        for head in range(HEADS):
-            score = scores[head * group_rows : (head + 1) * group_rows]
-            score = jnp.where(visible, score, masked_score)
-            lifted = jnp.exp2((score - jnp.max(score, axis=0, keepdims=True)) * factor)
-            scale = 1.0 / jnp.sum(lifted, axis=0, keepdims=True)
-            context.append(
-                jnp.dot(
-                    value[head * head_dim : (head + 1) * head_dim],
-                    (lifted * scale).astype(jnp.bfloat16),
-                    preferred_element_type=jnp.float32,
-                )
+        for at_pair in range(HEADS // 2):
+            product = jnp.dot(
+                value[at_pair * pair_dims : (at_pair + 1) * pair_dims],
+                shares[:, at_pair * pair : (at_pair + 1) * pair],
+                preferred_element_type=jnp.float32,
             )
-        context = jnp.transpose(jnp.concatenate(context, axis=0).astype(jnp.bfloat16))
-        result = before[at] + jnp.dot(context, weights[5], preferred_element_type=jnp.float32)
-        results.append(result.reshape(snaps, 1, SUBLANES, width))
-    evolved = jnp.concatenate(results, axis=1).reshape(n_snap, snap_dev, vert_dev, width)
-
-    low = lax.broadcasted_iota(jnp.int32, (n_snap * vert_dev, LANES), 1) < feat_width
+            context.append(jnp.where(pair_row == pair_col, product, 0.0).astype(jnp.bfloat16))
+        contexts.append(jnp.transpose(jnp.concatenate(context, axis=0)))
+    mixed = jnp.dot(
+        jnp.concatenate(contexts, axis=0), weights[5], preferred_element_type=jnp.float32
+    ).reshape(groups, 2, group_rows, width)
+    results = [
+        (before[at] + (mixed[at, 0] + mixed[at, 1])).reshape(half_snaps, 1, SUBLANES, width)
+        for at in range(groups)
+    ]
+    half_dev = n_snap // 2
+    evolved = jnp.concatenate(results, axis=1).reshape(half_dev, snap_dev, vert_dev, width)
+
+    low = lax.broadcasted_iota(jnp.int32, (half_dev * vert_dev, LANES), 1) < feat_width
     for at in range(0, n_feat, 2):
         lanes = slice(at * feat_width, (at + 2) * feat_width)
-        first = evolved[:, 0, :, lanes].reshape(n_snap * vert_dev, LANES)
-        second = evolved[:, 1, :, lanes].reshape(n_snap * vert_dev, LANES)
+        first = evolved[:, 0, :, lanes].reshape(half_dev * vert_dev, LANES)
+        second = evolved[:, 1, :, lanes].reshape(half_dev * vert_dev, LANES)
         even = jnp.where(low, first, pltpu.roll(second, feat_width, 1))
         odd = jnp.where(low, pltpu.roll(first, feat_width, 1), second)
-        outgoing[at] = even.astype(jnp.bfloat16).reshape(n_snap, vert_dev, LANES)
-        outgoing[at + 1] = odd.astype(jnp.bfloat16).reshape(n_snap, vert_dev, LANES)
-
-    returns = []
+        outgoing[at] = even.astype(jnp.bfloat16).reshape(half_dev, vert_dev, LANES)
+        outgoing[at + 1] = odd.astype(jnp.bfloat16).reshape(half_dev, vert_dev, LANES)
+
+    total = half_dev * n_feat
+    me = (me_snap % half_dev) * n_feat + me_feat
     for step in sorted(range(1, total), key=lambda s: abs(2 * s - total)):
         peer = (me + step) % total
-        copy = pltpu.make_async_remote_copy(
+        pltpu.make_async_remote_copy(
             src_ref=outgoing.at[peer % n_feat, peer // n_feat],
-            dst_ref=returned.at[part, own],
-            send_sem=return_send.at[step],
-            recv_sem=return_recv.at[step],
-            device_id=(peer // n_feat, peer % n_feat),
+            dst_ref=returned.at[part, rank],
+            send_sem=return_send,
+            recv_sem=return_recv,
+            device_id=(half * half_dev + peer // n_feat, peer % n_feat),
             device_id_type=MESH,
-        )
-        copy.start()
-        returns.append(copy)
-    own_copy = load(outgoing.at[me_feat, me_snap], returned.at[part, own], 0)
-    for copy in gathers + sends:
-        copy.wait_send()
+        ).start()
+    own_copy = load(outgoing.at[me_feat, me_snap % half_dev], returned.at[part, rank], 0)
+    settle(pieces.at[pl.ds(0, n_feat - 1)], gather_send)
+
+    @pl.when(is_low)
+    def _():
+        settle(hidden_two.at[pl.ds(0, half_snaps)], spread_send.at[1])
+        settle(hidden_two.at[pl.ds(0, half_snaps - 1)], spread_send.at[0])
+
+    @pl.when(is_high)
+    def _():
+        settle(hidden_two.at[pl.ds(0, half_snaps - 1)], spread_send.at[1])
+
     own_copy.wait()
-    for copy in returns:
-        copy.wait_recv()
-    for copy in returns:
-        copy.wait_send()
+    everyone = outgoing.reshape(total, vert_dev, LANES).at[pl.ds(0, total - 1)]
+    settle(everyone, return_recv)
+    settle(everyone, return_send)
 
 
 def on_device_fused(n_snap, n_feat, *operands):
@@ -416,14 +488,14 @@
     width = layer_one.shape[0]
     parts = n_feat // snap_dev
     snaps = n_snap * snap_dev
-    vert_dev = vert_count // (parts * snaps)
-    total = n_snap * n_feat
+    half_snaps = snaps // 2
+    vert_dev = vert_count // (parts * half_snaps)
     kept = jnp.bfloat16
     result = pl.pallas_call(
         functools.partial(fused_kernel, n_snap, n_feat),
-        out_shape=jax.ShapeDtypeStruct((parts, snaps, vert_dev, LANES), kept),
+        out_shape=pltpu.VMEM((parts, half_snaps, vert_dev, LANES), kept),
         in_specs=[pl.BlockSpec(memory_space=pltpu.HBM)] * 11,
-        out_specs=pl.BlockSpec(memory_space=pl.ANY),
+        out_specs=pl.BlockSpec(memory_space=pltpu.VMEM),
         scratch_shapes=[
             pltpu.VMEM((slot_total, tile_side, tile_side), kept),
             pltpu.VMEM((6, width, width), kept),
@@ -431,17 +503,17 @@
             pltpu.VMEM((vert_count, vert_count), kept),
             pltpu.VMEM((vert_count, width), kept),
             pltpu.VMEM((vert_count, width), kept),
+            pltpu.VMEM((half_snaps, vert_dev, width), kept),
             pltpu.VMEM((snaps, vert_dev, width), kept),
-            pltpu.VMEM((snaps, vert_dev, width), kept),
-            pltpu.VMEM((n_feat, n_snap, vert_dev, LANES), kept),
-            pltpu.SemaphoreType.DMA((11,)),
-            pltpu.SemaphoreType.DMA((n_feat,)),
-            pltpu.SemaphoreType.DMA((n_feat,)),
-            pltpu.SemaphoreType.DMA((snaps,)),
-            pltpu.SemaphoreType.DMA((snaps,)),
-            pltpu.SemaphoreType.DMA((total,)),
-            pltpu.SemaphoreType.DMA((total,)),
-            pltpu.SemaphoreType.REGULAR((n_snap // 4 + 1,)),
+            pltpu.VMEM((n_feat, n_snap // 2, vert_dev, LANES), kept),
+            pltpu.SemaphoreType.DMA((6,)),
+            pltpu.SemaphoreType.DMA,
+            pltpu.SemaphoreType.DMA,
+            pltpu.SemaphoreType.DMA((2,)),
+            pltpu.SemaphoreType.DMA((2,)),
+            pltpu.SemaphoreType.DMA,
+            pltpu.SemaphoreType.DMA,
+            pltpu.SemaphoreType.REGULAR((n_snap // 2,)),
             pltpu.SMEM((snap_dev, slot_total), jnp.int32),
             pltpu.SMEM((snap_dev, slot_total), jnp.int32),
             pltpu.SMEM((snap_dev,), jnp.int32),
@@ -463,7 +535,7 @@
         and n_feat % 2 == 0
         and n_snap >= 8
         and n_snap % 4 == 0
-        and vert_count % (n_feat // snap_dev * snaps * 2 * SUBLANES) == 0
+        and vert_count % (n_feat // snap_dev * snaps * SUBLANES) == 0
         and snaps * SUBLANES == LANES
         and slot_total <= 16
         and vert_count <= 1024

time: 26.1 us -> 22.1 us (0.85)
  Pallas kernels: 24.3 us -> 21.2 us
  local copies, waits for them, and re-layouts: 1.67 us -> 0.77 us
    pallas_call x1, Pallas kernels: 24.3 us -> 21.2 us  [on_device_fused(): pl.pallas_call(functools.partial(fused_kernel, n_snap, n_feat), out_shape...]
    transpose x1, local copies, waits for them, and re-layouts: 1.67 us -> 0.77 us  [on_device_fused(): result = jnp.transpose(result.reshape(vert_count, LANES))]
where the time goes in v1:
time: 22.1 us; the launch traced here: 22 us
  Pallas kernels  21.2 us (96%)
  local copies, waits for them, and re-layouts  0.77 us (3%)
    pallas_call x1, Pallas kernels, on_device_fused(): pl.pallas_call(functools.partial(fused_kernel, n_snap, n_feat), out_shape...  21.2 us
    transpose x1, local copies, waits for them, and re-layouts, on_device_fused(): result = jnp.transpose(result.reshape(vert_count, LANES))  0.77 us

profile of v1, /device:TPU:0, one launch (start us, length us, event | category | flops | bytes accessed | tf_op | source)
XLA Modules:
  0.0 22.0 jit_solution(10979165077179183472)
XLA Ops:
  0.0 21.2 %shard_map.109 = bf16[2,8,32,128]{3,2,1,0:T(8,128)(2,1)S(1)} custom-call(s32[2,8]{1,0:T(2,128)} %rows_hbm.1, s32[2,8]{1,0:T(2,128)} %cols_hbm.1, s32[2]{0:T(128)} %counts_hbm.1, bf16[2,64,512]{2,1,0:T(8,128)(2,1)} %bitcast.8, bf16[2,8,128,128]{3,2,1,0:T(8,128)(2,1)} %tiles_ref.1, bf16[256,256]{1,0:T(8,128)(2,1)} %w_one.1, bf16[256,256]{1,0:T(8,128)(2,1)} %w_two.1, ...), custom_call_target="tpu_custom_call" | custom-call | tf_op jit(solution)/shard_map/pallas_call | solution.py:494
  21.2 0.8 %copy.12 = bf16[128,512]{1,0:T(8,128)(2,1)} copy(bf16[128,512]{0,1:T(8,128)(2,1)S(1)} %bitcast.7) | data formatting | bytes 262144 | tf_op jit(solution)/shard_map/transpose | solution.py:523

commit v2 on v1

--- a/solution.py
+++ b/solution.py
@@ -134,6 +134,7 @@
 
 
 LANES = 128
+CHUNKS = 4
 SUBLANES = 8
 MESH = pl.DeviceIdType.MESH
 
@@ -237,26 +238,46 @@
     tile_load = load(tiles_ref.at[local], tiles, 1)
     pl.semaphore_wait(barrier, n_feat + column_count)
 
-    for step in [n_feat // 2] + [s for s in range(1, n_feat) if s != n_feat // 2]:
-        peer = (me_feat + step) % n_feat
+    partner = (me_feat + parts) % n_feat
+    mate = local * parts + 1 - part
+    chunk = feat_width // CHUNKS
+    spans = [pl.ds(at * chunk, chunk) for at in range(CHUNKS)]
+    for at in range(CHUNKS):
         pltpu.make_async_remote_copy(
-            src_ref=feat_ref.at[peer // parts],
-            dst_ref=pieces.at[me_feat],
+            src_ref=feat_ref.at[partner // parts, spans[at]],
+            dst_ref=pieces.at[me_feat, spans[at]],
             send_sem=gather_send,
-            recv_sem=gather_recv,
-            device_id=(me_snap, peer),
+            recv_sem=gather_recv.at[at],
+            device_id=(me_snap, partner),
             device_id_type=MESH,
         ).start()
+    pltpu.make_async_remote_copy(
+        src_ref=feat_ref.at[local],
+        dst_ref=pieces.at[me_feat],
+        send_sem=gather_send,
+        recv_sem=gather_recv.at[CHUNKS],
+        device_id=(me_snap, mate),
+        device_id_type=MESH,
+    ).start()
+
+    def relay(at):
+        passed = pieces.at[partner, spans[at]]
+        settle(passed, gather_recv.at[at])
+        pltpu.make_async_remote_copy(
+            src_ref=passed,
+            dst_ref=passed,
+            send_sem=gather_send,
+            recv_sem=gather_recv.at[CHUNKS],
+            device_id=(me_snap, mate),
+            device_id_type=MESH,
+        ).start()
+
     for at, ref in enumerate((w_one, w_two, w_query, w_key, w_value, w_out)):
         load(ref, weights.at[at], 5)
     own_load = load(feat_ref.at[local], pieces.at[me_feat], 0)
 
     hops = n_snap // plane - 2
-    for hop in range(hops):
-        tell_column(heard.at[hop])
-        if hop + 1 < hops:
-            pl.semaphore_wait(heard.at[hop], column_count)
-
+    tell_column(heard.at[0])
     tile_load.wait()
     for copy in list_loads:
         copy.wait()
@@ -288,14 +309,19 @@
 
     strips = tile_side // strip
     lax.fori_loop(0, strips // 2, build, 0)
+    for hop in range(hops - 1):
+        pl.semaphore_wait(heard.at[hop], column_count)
+        tell_column(heard.at[hop + 1])
+    lax.fori_loop(strips // 2, strips, build, 0)
     pl.semaphore_wait(heard.at[hops - 1], column_count)
     signal(heard.at[hops], (twin, me_feat))
-    lax.fori_loop(strips // 2, strips, build, 0)
+    for at in range(CHUNKS):
+        relay(at)
     pl.semaphore_wait(heard.at[hops], 1)
     tell_mates(heard.at[hops + 1])
 
     settle(weights, load_sem.at[5])
-    settle(pieces.at[pl.ds(0, n_feat - 1)], gather_recv)
+    settle(pieces.at[pl.ds(0, n_feat // 2)], gather_recv.at[CHUNKS])
     own_load.wait()
     features[...] = jnp.transpose(pieces[...].reshape(width, vert_count))
 
@@ -320,26 +346,29 @@
             device_id_type=MESH,
         ).start()
 
+    def flip(index, mask):
+        flipped = 0
+        for bit in (4, 2, 1):
+            digit = index // bit % 2
+            flipped = flipped + bit * (1 - digit if mask & bit else digit)
+        return flipped
+
     def spread_half(target_half):
-        for step in [half_snaps // 2] + [
-            s for s in range(1, half_snaps) if s != half_snaps // 2
-        ]:
-            spread_to(target_half, (rank + step) % half_snaps)
-
+        for mask in (7, 6, 5, 3, 4, 2, 1):
+            spread_to(target_half, flip(rank, mask))
+
+    near = rank % (half_snaps // 2)
     own_rows = pl.ds(pl.multiple_of(part * part_rows, part_rows), part_rows)
     hidden_two[...] = mix(
         adjacency[own_rows, :], hidden_one[...], hidden_one[own_rows, :], weights[1]
     ).reshape(half_snaps, vert_dev, width)
-    side = half_snaps // 2
-    far = [side + (rank + step) % side for step in range(side)]
-    near = [(rank + step) % side for step in range(side)]
 
     @pl.when(is_low)
     def _():
         spread_half(0)
-        for peer in far + near:
-            spread_to(1, peer)
-
+        for high in (1, 0):
+            for mask in (3, 2, 1, 0):
+                spread_to(1, high * (half_snaps // 2) + flip(near, mask))
     @pl.when(is_high)
     def _():
         spread_half(1)
@@ -348,7 +377,11 @@
 
     groups = vert_dev // SUBLANES
     group_rows = half_snaps * SUBLANES
-    columns = HEADS * group_rows
+    pair = 2 * group_rows
+    pair_dims = 2 * head_dim
+    quads = width // LANES
+    quad_pairs = LANES // pair_dims
+    half_dev = n_snap // 2
 
     def split(array):
         array = array.reshape(half_snaps, groups, SUBLANES, width)
@@ -357,104 +390,142 @@
     def project(flat, at):
         return split(jnp.dot(flat, weights[at], preferred_element_type=jnp.float32))
 
-    def score(keys, queries):
-        return lax.dot_general(
-            keys.astype(jnp.bfloat16),
-            queries,
-            (((1,), (1,)), ((), ())),
-            preferred_element_type=jnp.float32,
-        )
-
-    row_at = lax.broadcasted_iota(jnp.int32, (group_rows, columns), 0)
-    col_at = lax.broadcasted_iota(jnp.int32, (group_rows, columns), 1) % group_rows
+    def score(keys, turned):
+        keys = keys.astype(jnp.bfloat16)
+        return [
+            jnp.dot(
+                keys[:, at * LANES : (at + 1) * LANES],
+                turned[at],
+                preferred_element_type=jnp.float32,
+            )
+            for at in range(quads)
+        ]
+
+    quad_columns = quad_pairs * pair
+    row_at = lax.broadcasted_iota(jnp.int32, (group_rows, quad_columns), 0)
+    col_at = lax.broadcasted_iota(jnp.int32, (group_rows, quad_columns), 1) % group_rows
     same = row_at % SUBLANES == col_at % SUBLANES
     visible = same & (row_at // SUBLANES <= col_at // SUBLANES)
-    visible_low = same & (jnp.full((group_rows, columns), half, jnp.int32) == 1)
-    lane_head = lax.broadcasted_iota(jnp.int32, (group_rows, width), 1) // head_dim
     factor = head_dim ** (-0.5) * math.log2(math.e)
+    none = jnp.zeros((pair_dims, pair), jnp.bfloat16)
+    ones = jnp.ones((2 * SUBLANES, group_rows), jnp.bfloat16)
 
     settle(vertex_rows.at[pl.ds(0, half_snaps - 1)], spread_recv.at[half])
     own_rows = vertex_rows[pl.ds(half * half_snaps, half_snaps)]
     flat = own_rows.reshape(half_snaps * vert_dev, width)
-    before = split(flat.astype(jnp.float32))
-    queries = [
-        jnp.concatenate(
+    doubled = jnp.concatenate(
+        [query for query in project(flat, 2) for _ in range(2)], axis=0
+    )
+    turned = jnp.transpose(doubled.astype(jnp.bfloat16))
+    turned_head = lax.broadcasted_iota(jnp.int32, turned.shape, 0) // head_dim
+    turned_side = lax.broadcasted_iota(jnp.int32, turned.shape, 1) // group_rows
+    turned = jnp.where(turned_head % 2 == turned_side % 2, turned, 0.0)
+    queries = []
+    for at in range(groups):
+        columns = turned[:, at * pair : (at + 1) * pair]
+        queries.append(
             [
-                jnp.where(lane_head == head, query, 0.0).astype(jnp.bfloat16)
-                for head in range(HEADS)
-            ],
-            axis=0,
+                jnp.concatenate(
+                    [
+                        jnp.concatenate(
+                            [
+                                columns[
+                                    (quad * quad_pairs + inner) * pair_dims : (
+                                        quad * quad_pairs + inner + 1
+                                    )
+                                    * pair_dims
+                                ]
+                                if inner == outer
+                                else none
+                                for inner in range(quad_pairs)
+                            ],
+                            axis=0,
+                        )
+                        for outer in range(quad_pairs)
+                    ],
+                    axis=1,
+                )
+                for quad in range(quads)
+            ]
         )
-        for query in project(flat, 2)
-    ]
     keys, values = project(flat, 3), project(flat, 4)
     scores = [
-        jnp.where(visible, score(keys[at], queries[at]), masked_score)
+        [jnp.where(visible, each, masked_score) for each in score(keys[at], queries[at])]
         for at in range(groups)
     ]
+
+    def attend(scores_of, values_of):
+        lane_odd = lax.broadcasted_iota(jnp.int32, (group_rows, width), 1) // head_dim % 2 == 1
+        contexts = []
+        for at in range(groups):
+            value = jnp.transpose(
+                jnp.concatenate([each[at] for each in values_of], axis=0).astype(jnp.bfloat16)
+            )
+            tail = jnp.concatenate([ones] * len(values_of), axis=1)
+            context = []
+            for quad in range(quads):
+                listed = [each[at][quad] for each in scores_of]
+                highest = functools.reduce(
+                    jnp.maximum, [jnp.max(each, axis=0, keepdims=True) for each in listed]
+                )
+                shares = jnp.concatenate(
+                    [
+                        jnp.exp2((each - highest) * factor).astype(jnp.bfloat16)
+                        for each in listed
+                    ],
+                    axis=0,
+                )
+                for inner in range(quad_pairs):
+                    first = (quad * quad_pairs + inner) * pair_dims
+                    product = jnp.dot(
+                        jnp.concatenate([value[first : first + pair_dims], tail], axis=0),
+                        shares[:, inner * pair : (inner + 1) * pair],
+                        preferred_element_type=jnp.float32,
+                    )
+                    scale = 1.0 / product[pair_dims : pair_dims + 1]
+                    context.append((product[:pair_dims] * scale).astype(jnp.bfloat16))
+            context = jnp.transpose(jnp.concatenate(context, axis=0))
+            contexts.append(jnp.where(lane_odd, context[group_rows:], context[:group_rows]))
+        mixed = jnp.dot(
+            jnp.concatenate(contexts, axis=0), weights[5], preferred_element_type=jnp.float32
+        ).reshape(groups, half_snaps, SUBLANES, width)
+        before = own_rows.astype(jnp.float32).reshape(half_snaps, groups, SUBLANES, width)
+        evolved = jnp.concatenate(
+            [
+                before[:, at : at + 1] + mixed[at].reshape(half_snaps, 1, SUBLANES, width)
+                for at in range(groups)
+            ],
+            axis=1,
+        ).reshape(half_dev, snap_dev, vert_dev, width)
+        low = lax.broadcasted_iota(jnp.int32, (half_dev * vert_dev, LANES), 1) < feat_width
+        for at in range(0, n_feat, 2):
+            lanes = slice(at * feat_width, (at + 2) * feat_width)
+            first = evolved[:, 0, :, lanes].reshape(half_dev * vert_dev, LANES)
+            second = evolved[:, 1, :, lanes].reshape(half_dev * vert_dev, LANES)
+            even = jnp.where(low, first, pltpu.roll(second, feat_width, 1))
+            odd = jnp.where(low, pltpu.roll(first, feat_width, 1), second)
+            outgoing[at] = even.astype(jnp.bfloat16).reshape(half_dev, vert_dev, LANES)
+            outgoing[at + 1] = odd.astype(jnp.bfloat16).reshape(half_dev, vert_dev, LANES)
+
+    @pl.when(is_low)
+    def _():
+        attend([scores], [values])
 
     @pl.when(is_high)
     def _():
         settle(vertex_rows.at[pl.ds(0, half_snaps)], spread_recv.at[0])
-
-    flat_low = vertex_rows[pl.ds(0, half_snaps)].reshape(half_snaps * vert_dev, width)
-    keys_low, values_low = project(flat_low, 3), project(flat_low, 4)
-    pair = 2 * group_rows
-    pair_dims = 2 * head_dim
-    pair_row = lax.broadcasted_iota(jnp.int32, (pair_dims, pair), 0) // head_dim
-    pair_col = lax.broadcasted_iota(jnp.int32, (pair_dims, pair), 1) // group_rows
-    contexts = []
-    for at in range(groups):
-        score_low = jnp.where(visible_low, score(keys_low[at], queries[at]), masked_score)
-        score_own = scores[at]
-        highest = jnp.maximum(
-            jnp.max(score_low, axis=0, keepdims=True), jnp.max(score_own, axis=0, keepdims=True)
-        )
-        lifted_low = jnp.exp2((score_low - highest) * factor)
-        lifted_own = jnp.exp2((score_own - highest) * factor)
-        scale = 1.0 / (
-            jnp.sum(lifted_low, axis=0, keepdims=True) + jnp.sum(lifted_own, axis=0, keepdims=True)
-        )
-        shares = jnp.concatenate(
-            [(lifted_low * scale).astype(jnp.bfloat16), (lifted_own * scale).astype(jnp.bfloat16)],
-            axis=0,
-        )
-        value = jnp.transpose(
-            jnp.concatenate([values_low[at], values[at]], axis=0).astype(jnp.bfloat16)
-        )
-        context = []
-        for at_pair in range(HEADS // 2):
-            product = jnp.dot(
-                value[at_pair * pair_dims : (at_pair + 1) * pair_dims],
-                shares[:, at_pair * pair : (at_pair + 1) * pair],
-                preferred_element_type=jnp.float32,
-            )
-            context.append(jnp.where(pair_row == pair_col, product, 0.0).astype(jnp.bfloat16))
-        contexts.append(jnp.transpose(jnp.concatenate(context, axis=0)))
-    mixed = jnp.dot(
-        jnp.concatenate(contexts, axis=0), weights[5], preferred_element_type=jnp.float32
-    ).reshape(groups, 2, group_rows, width)
-    results = [
-        (before[at] + (mixed[at, 0] + mixed[at, 1])).reshape(half_snaps, 1, SUBLANES, width)
-        for at in range(groups)
-    ]
-    half_dev = n_snap // 2
-    evolved = jnp.concatenate(results, axis=1).reshape(half_dev, snap_dev, vert_dev, width)
-
-    low = lax.broadcasted_iota(jnp.int32, (half_dev * vert_dev, LANES), 1) < feat_width
-    for at in range(0, n_feat, 2):
-        lanes = slice(at * feat_width, (at + 2) * feat_width)
-        first = evolved[:, 0, :, lanes].reshape(half_dev * vert_dev, LANES)
-        second = evolved[:, 1, :, lanes].reshape(half_dev * vert_dev, LANES)
-        even = jnp.where(low, first, pltpu.roll(second, feat_width, 1))
-        odd = jnp.where(low, pltpu.roll(first, feat_width, 1), second)
-        outgoing[at] = even.astype(jnp.bfloat16).reshape(half_dev, vert_dev, LANES)
-        outgoing[at + 1] = odd.astype(jnp.bfloat16).reshape(half_dev, vert_dev, LANES)
+        flat_low = vertex_rows[pl.ds(0, half_snaps)].reshape(half_snaps * vert_dev, width)
+        keys_low, values_low = project(flat_low, 3), project(flat_low, 4)
+        scores_low = [
+            [jnp.where(same, each, masked_score) for each in score(keys_low[at], queries[at])]
+            for at in range(groups)
+        ]
+        attend([scores_low, scores], [values_low, values])
 
     total = half_dev * n_feat
     me = (me_snap % half_dev) * n_feat + me_feat
-    for step in sorted(range(1, total), key=lambda s: abs(2 * s - total)):
-        peer = (me + step) % total
+    for mask in (14, 15, 12, 13, 10, 11, 6, 7, 8, 9, 4, 5, 2, 3, 1):
+        peer = flip(me // 2, mask // 2) * 2 + (1 - me % 2 if mask % 2 else me % 2)
         pltpu.make_async_remote_copy(
             src_ref=outgoing.at[peer % n_feat, peer // n_feat],
             dst_ref=returned.at[part, rank],
@@ -508,7 +579,7 @@
             pltpu.VMEM((n_feat, n_snap // 2, vert_dev, LANES), kept),
             pltpu.SemaphoreType.DMA((6,)),
             pltpu.SemaphoreType.DMA,
-            pltpu.SemaphoreType.DMA,
+            pltpu.SemaphoreType.DMA((CHUNKS + 1,)),
             pltpu.SemaphoreType.DMA((2,)),
             pltpu.SemaphoreType.DMA((2,)),
             pltpu.SemaphoreType.DMA,
@@ -531,8 +602,7 @@
     fits = (
         snap_dev == 2
         and 2 * feat_width == LANES
-        and n_feat % snap_dev == 0
-        and n_feat % 2 == 0
+        and n_feat == 2 * snap_dev
         and n_snap >= 8
         and n_snap % 4 == 0
         and vert_count % (n_feat // snap_dev * snaps * SUBLANES) == 0

time: 22.1 us -> 21 us (0.950)
  the two profiles are of different devices: /device:TPU:0 before, /device:TPU:17 now
where the time goes in v2:
time: 21 us; the launch traced here: 20.9 us
  Pallas kernels  20.1 us (96%)
  local copies, waits for them, and re-layouts  0.77 us (4%)
    pallas_call x1, Pallas kernels, on_device_fused(): pl.pallas_call(functools.partial(fused_kernel, n_snap, n_feat), out_shape...  20.1 us
    transpose x1, local copies, waits for them, and re-layouts, on_device_fused(): result = jnp.transpose(result.reshape(vert_count, LANES))  0.77 us

profile of v2, /device:TPU:17, one launch (start us, length us, event | category | flops | bytes accessed | tf_op | source)
XLA Modules:
  0.0 20.9 jit_solution(2739872105654518117)
XLA Ops:
  0.0 20.1 %shard_map.109 = bf16[2,8,32,128]{3,2,1,0:T(8,128)(2,1)S(1)} custom-call(s32[2,8]{1,0:T(2,128)} %rows_hbm.1, s32[2,8]{1,0:T(2,128)} %cols_hbm.1, s32[2]{0:T(128)} %counts_hbm.1, bf16[2,64,512]{2,1,0:T(8,128)(2,1)} %bitcast.8, bf16[2,8,128,128]{3,2,1,0:T(8,128)(2,1)} %tiles_ref.1, bf16[256,256]{1,0:T(8,128)(2,1)} %w_one.1, bf16[256,256]{1,0:T(8,128)(2,1)} %w_two.1, ...), custom_call_target="tpu_custom_call" | custom-call | tf_op jit(solution)/shard_map/pallas_call | solution.py:565
  20.1 0.8 %copy.12 = bf16[128,512]{1,0:T(8,128)(2,1)} copy(bf16[128,512]{0,1:T(8,128)(2,1)S(1)} %bitcast.7) | data formatting | bytes 262144 | tf_op jit(solution)/shard_map/transpose | solution.py:594

commit v3 on v2

--- a/solution.py
+++ b/solution.py
@@ -134,7 +134,7 @@
 
 
 LANES = 128
-CHUNKS = 4
+CHUNKS = 2
 SUBLANES = 8
 MESH = pl.DeviceIdType.MESH
 
@@ -156,6 +156,7 @@
     returned,
     tiles,
     weights,
+    away,
     pieces,
     adjacency,
     features,
@@ -163,6 +164,7 @@
     hidden_two,
     vertex_rows,
     outgoing,
+    lending,
     load_sem,
     gather_send,
     gather_recv,
@@ -210,25 +212,36 @@
     has_above = me_snap < n_snap - plane
     column_count = has_below.astype(jnp.int32) + has_above.astype(jnp.int32)
 
+    lead = local * parts + parts - 1
+
     def signal(semaphore, peer):
         pl.semaphore_signal(semaphore, inc=1, device_id=peer, device_id_type=MESH)
 
     def tell_column(semaphore):
         @pl.when(has_below)
         def _():
-            signal(semaphore, (me_snap - plane, me_feat))
+            signal(semaphore, (me_snap - plane, lead))
 
         @pl.when(has_above)
         def _():
-            signal(semaphore, (me_snap + plane, me_feat))
+            signal(semaphore, (me_snap + plane, lead))
 
     def tell_mates(semaphore):
         for mate in mates:
             signal(semaphore, (me_snap, mate))
 
+    leads = part == parts - 1
+    lead_count = leads.astype(jnp.int32)
     tell_mates(barrier)
-    signal(barrier, (twin, me_feat))
     tell_column(barrier)
+
+    @pl.when(leads)
+    def _():
+        signal(barrier, (twin, me_feat))
+
+    partner = (me_feat + parts) % n_feat
+    away_load = load(feat_ref.at[partner // parts], away, 6)
+    own_load = load(feat_ref.at[local], pieces.at[me_feat], 0)
     list_loads = [
         load(ref, kept, 2 + at)
         for at, (ref, kept) in enumerate(
@@ -236,29 +249,32 @@
         )
     ]
     tile_load = load(tiles_ref.at[local], tiles, 1)
-    pl.semaphore_wait(barrier, n_feat + column_count)
-
-    partner = (me_feat + parts) % n_feat
+    weight_list = (w_one, w_two, w_query, w_key, w_value, w_out)
+    pl.semaphore_wait(barrier, len(mates) + lead_count * (1 + parts * column_count))
+
     mate = local * parts + 1 - part
-    chunk = feat_width // CHUNKS
+    across = (partner // parts) * parts + 1 - part
+    chunk = feat_width // (2 * CHUNKS)
     spans = [pl.ds(at * chunk, chunk) for at in range(CHUNKS)]
-    for at in range(CHUNKS):
+    rest = pl.ds(feat_width // 2, feat_width // 2)
+
+    def gather(source, span, at, peer):
         pltpu.make_async_remote_copy(
-            src_ref=feat_ref.at[partner // parts, spans[at]],
-            dst_ref=pieces.at[me_feat, spans[at]],
+            src_ref=source.at[span],
+            dst_ref=pieces.at[me_feat, span],
             send_sem=gather_send,
             recv_sem=gather_recv.at[at],
-            device_id=(me_snap, partner),
+            device_id=(me_snap, peer),
             device_id_type=MESH,
         ).start()
-    pltpu.make_async_remote_copy(
-        src_ref=feat_ref.at[local],
-        dst_ref=pieces.at[me_feat],
-        send_sem=gather_send,
-        recv_sem=gather_recv.at[CHUNKS],
-        device_id=(me_snap, mate),
-        device_id_type=MESH,
-    ).start()
+
+    away_load.wait()
+    for at in range(CHUNKS):
+        gather(away, spans[at], at, partner)
+    gather(away, rest, CHUNKS, partner)
+    gather(away, rest, CHUNKS, across)
+    own_load.wait()
+    gather(pieces.at[me_feat], pl.ds(0, feat_width), CHUNKS, mate)
 
     def relay(at):
         passed = pieces.at[partner, spans[at]]
@@ -272,12 +288,15 @@
             device_id_type=MESH,
         ).start()
 
-    for at, ref in enumerate((w_one, w_two, w_query, w_key, w_value, w_out)):
+    for at, ref in enumerate(weight_list):
         load(ref, weights.at[at], 5)
-    own_load = load(feat_ref.at[local], pieces.at[me_feat], 0)
 
     hops = n_snap // plane - 2
-    tell_column(heard.at[0])
+
+    @pl.when(leads)
+    def _():
+        tell_column(heard.at[0])
+
     tile_load.wait()
     for copy in list_loads:
         copy.wait()
@@ -310,19 +329,30 @@
     strips = tile_side // strip
     lax.fori_loop(0, strips // 2, build, 0)
     for hop in range(hops - 1):
-        pl.semaphore_wait(heard.at[hop], column_count)
-        tell_column(heard.at[hop + 1])
+
+        @pl.when(leads)
+        def _():
+            pl.semaphore_wait(heard.at[hop], column_count)
+            tell_column(heard.at[hop + 1])
+
     lax.fori_loop(strips // 2, strips, build, 0)
-    pl.semaphore_wait(heard.at[hops - 1], column_count)
-    signal(heard.at[hops], (twin, me_feat))
+
+    @pl.when(leads)
+    def _():
+        pl.semaphore_wait(heard.at[hops - 1], column_count)
+        signal(heard.at[hops], (twin, me_feat))
+
     for at in range(CHUNKS):
         relay(at)
-    pl.semaphore_wait(heard.at[hops], 1)
-    tell_mates(heard.at[hops + 1])
+
+    @pl.when(leads)
+    def _():
+        pl.semaphore_wait(heard.at[hops], 1)
+        tell_mates(heard.at[hops + 1])
+
 
     settle(weights, load_sem.at[5])
-    settle(pieces.at[pl.ds(0, n_feat // 2)], gather_recv.at[CHUNKS])
-    own_load.wait()
+    settle(pieces.at[:, pl.ds(0, 5 * feat_width // 8)], gather_recv.at[CHUNKS])
     features[...] = jnp.transpose(pieces[...].reshape(width, vert_count))
 
     def mix(lhs, source, before, weight):
@@ -333,13 +363,17 @@
         return (before.astype(jnp.float32) + jnp.maximum(mixed, 0.0)).astype(jnp.bfloat16)
 
     hidden_one[...] = mix(adjacency[...], features[...], features[...], weights[0])
-    pl.semaphore_wait(heard.at[hops + 1], len(mates))
-
-    def spread_to(target_half, peer):
+    pl.semaphore_wait(heard.at[hops + 1], snap_dev - lead_count)
+
+    kept_rows = pl.ds(0, vert_dev - SUBLANES)
+    lent_rows = pl.ds(vert_dev - SUBLANES, SUBLANES)
+    all_rows = pl.ds(0, vert_dev)
+
+    def spread_to(target_half, peer, rows):
         target = target_half * half_snaps + peer
         pltpu.make_async_remote_copy(
-            src_ref=hidden_two.at[peer],
-            dst_ref=vertex_rows.at[own],
+            src_ref=hidden_two.at[peer, rows],
+            dst_ref=vertex_rows.at[own, rows],
             send_sem=spread_send.at[target_half],
             recv_sem=spread_recv.at[half],
             device_id=(target // snap_dev, (target % snap_dev) * parts + part),
@@ -353,9 +387,9 @@
             flipped = flipped + bit * (1 - digit if mask & bit else digit)
         return flipped
 
-    def spread_half(target_half):
+    def spread_half(target_half, rows):
         for mask in (7, 6, 5, 3, 4, 2, 1):
-            spread_to(target_half, flip(rank, mask))
+            spread_to(target_half, flip(rank, mask), rows)
 
     near = rank % (half_snaps // 2)
     own_rows = pl.ds(pl.multiple_of(part * part_rows, part_rows), part_rows)
@@ -365,13 +399,16 @@
 
     @pl.when(is_low)
     def _():
-        spread_half(0)
+        spread_half(0, all_rows)
         for high in (1, 0):
             for mask in (3, 2, 1, 0):
-                spread_to(1, high * (half_snaps // 2) + flip(near, mask))
+                spread_to(1, high * (half_snaps // 2) + flip(near, mask), kept_rows)
     @pl.when(is_high)
     def _():
-        spread_half(1)
+        for high in (0, 1):
+            for mask in (3, 2, 1, 0):
+                spread_to(0, high * (half_snaps // 2) + flip(near, mask), lent_rows)
+        spread_half(1, kept_rows)
 
     vertex_rows[own] = hidden_two[rank]
 
@@ -384,8 +421,8 @@
     half_dev = n_snap // 2
 
     def split(array):
-        array = array.reshape(half_snaps, groups, SUBLANES, width)
-        return [array[:, at].reshape(group_rows, width) for at in range(groups)]
+        array = array.reshape(half_snaps, -1, SUBLANES, width)
+        return [array[:, at].reshape(group_rows, width) for at in range(array.shape[1])]
 
     def project(flat, at):
         return split(jnp.dot(flat, weights[at], preferred_element_type=jnp.float32))
@@ -410,54 +447,46 @@
     none = jnp.zeros((pair_dims, pair), jnp.bfloat16)
     ones = jnp.ones((2 * SUBLANES, group_rows), jnp.bfloat16)
 
-    settle(vertex_rows.at[pl.ds(0, half_snaps - 1)], spread_recv.at[half])
-    own_rows = vertex_rows[pl.ds(half * half_snaps, half_snaps)]
-    flat = own_rows.reshape(half_snaps * vert_dev, width)
-    doubled = jnp.concatenate(
-        [query for query in project(flat, 2) for _ in range(2)], axis=0
-    )
-    turned = jnp.transpose(doubled.astype(jnp.bfloat16))
-    turned_head = lax.broadcasted_iota(jnp.int32, turned.shape, 0) // head_dim
-    turned_side = lax.broadcasted_iota(jnp.int32, turned.shape, 1) // group_rows
-    turned = jnp.where(turned_head % 2 == turned_side % 2, turned, 0.0)
-    queries = []
-    for at in range(groups):
-        columns = turned[:, at * pair : (at + 1) * pair]
-        queries.append(
-            [
-                jnp.concatenate(
-                    [
-                        jnp.concatenate(
-                            [
-                                columns[
-                                    (quad * quad_pairs + inner) * pair_dims : (
-                                        quad * quad_pairs + inner + 1
-                                    )
-                                    * pair_dims
-                                ]
-                                if inner == outer
-                                else none
-                                for inner in range(quad_pairs)
-                            ],
-                            axis=0,
-                        )
-                        for outer in range(quad_pairs)
-                    ],
-                    axis=1,
-                )
-                for quad in range(quads)
+    def masked(keys, queries, seen):
+        return [jnp.where(seen, each, masked_score) for each in score(keys, queries)]
+
+    def turn(listed):
+        doubled = jnp.concatenate([query for query in listed for _ in range(2)], axis=0)
+        turned = jnp.transpose(doubled.astype(jnp.bfloat16))
+        turned_head = lax.broadcasted_iota(jnp.int32, turned.shape, 0) // head_dim
+        turned_side = lax.broadcasted_iota(jnp.int32, turned.shape, 1) // group_rows
+        turned = jnp.where(turned_head % 2 == turned_side % 2, turned, 0.0)
+        queries = []
+        for at in range(len(listed)):
+            columns = turned[:, at * pair : (at + 1) * pair]
+            pairs = [
+                columns[first : first + pair_dims] for first in range(0, width, pair_dims)
             ]
-        )
-    keys, values = project(flat, 3), project(flat, 4)
-    scores = [
-        [jnp.where(visible, each, masked_score) for each in score(keys[at], queries[at])]
-        for at in range(groups)
-    ]
-
-    def attend(scores_of, values_of):
+            queries.append(
+                [
+                    jnp.concatenate(
+                        [
+                            jnp.concatenate(
+                                [
+                                    pairs[quad * quad_pairs + inner] if inner == outer else none
+                                    for inner in range(quad_pairs)
+                                ],
+                                axis=0,
+                            )
+                            for outer in range(quad_pairs)
+                        ],
+                        axis=1,
+                    )
+                    for quad in range(quads)
+                ]
+            )
+        return queries
+
+    def attend(scores_of, values_of, before):
         lane_odd = lax.broadcasted_iota(jnp.int32, (group_rows, width), 1) // head_dim % 2 == 1
+        count = len(before)
         contexts = []
-        for at in range(groups):
+        for at in range(count):
             value = jnp.transpose(
                 jnp.concatenate([each[at] for each in values_of], axis=0).astype(jnp.bfloat16)
             )
@@ -488,68 +517,116 @@
             contexts.append(jnp.where(lane_odd, context[group_rows:], context[:group_rows]))
         mixed = jnp.dot(
             jnp.concatenate(contexts, axis=0), weights[5], preferred_element_type=jnp.float32
-        ).reshape(groups, half_snaps, SUBLANES, width)
-        before = own_rows.astype(jnp.float32).reshape(half_snaps, groups, SUBLANES, width)
+        ).reshape(count, group_rows, width)
+        verts = count * SUBLANES
         evolved = jnp.concatenate(
             [
-                before[:, at : at + 1] + mixed[at].reshape(half_snaps, 1, SUBLANES, width)
-                for at in range(groups)
+                (before[at] + mixed[at]).reshape(half_snaps, 1, SUBLANES, width)
+                for at in range(count)
             ],
             axis=1,
-        ).reshape(half_dev, snap_dev, vert_dev, width)
-        low = lax.broadcasted_iota(jnp.int32, (half_dev * vert_dev, LANES), 1) < feat_width
+        ).reshape(half_dev, snap_dev, verts, width)
+        low = lax.broadcasted_iota(jnp.int32, (half_dev * verts, LANES), 1) < feat_width
+        outs = []
         for at in range(0, n_feat, 2):
             lanes = slice(at * feat_width, (at + 2) * feat_width)
-            first = evolved[:, 0, :, lanes].reshape(half_dev * vert_dev, LANES)
-            second = evolved[:, 1, :, lanes].reshape(half_dev * vert_dev, LANES)
+            first = evolved[:, 0, :, lanes].reshape(half_dev * verts, LANES)
+            second = evolved[:, 1, :, lanes].reshape(half_dev * verts, LANES)
             even = jnp.where(low, first, pltpu.roll(second, feat_width, 1))
             odd = jnp.where(low, pltpu.roll(first, feat_width, 1), second)
-            outgoing[at] = even.astype(jnp.bfloat16).reshape(half_dev, vert_dev, LANES)
-            outgoing[at + 1] = odd.astype(jnp.bfloat16).reshape(half_dev, vert_dev, LANES)
+            outs += [each.reshape(half_dev, verts, LANES) for each in (even, odd)]
+        return outs
+
+    total = half_dev * n_feat
+    me = (me_snap % half_dev) * n_feat + me_feat
+
+    def hand_back(source, target_half, peer, rows, source_rows, at):
+        pltpu.make_async_remote_copy(
+            src_ref=source.at[peer % n_feat, peer // n_feat, source_rows],
+            dst_ref=returned.at[part, rank, rows],
+            send_sem=return_send.at[at],
+            recv_sem=return_recv.at[at],
+            device_id=(target_half * half_dev + peer // n_feat, peer % n_feat),
+            device_id_type=MESH,
+        ).start()
+
+    masks = (14, 15, 12, 13, 10, 11, 6, 7, 8, 9, 4, 5, 2, 3, 1, 0)
+    mirrored = [
+        flip(me // 2, mask // 2) * 2 + (1 - me % 2 if mask % 2 else me % 2) for mask in masks
+    ]
+
+    def own_part(rows):
+        flat = rows.reshape(half_snaps * vert_dev, width)
+        return project(flat, 2), project(flat, 3), project(flat, 4), split(flat.astype(jnp.float32))
 
     @pl.when(is_low)
     def _():
-        attend([scores], [values])
+        settle(vertex_rows.at[pl.ds(0, half_snaps - 1)], spread_recv.at[0])
+        queries, keys, values, before = own_part(vertex_rows[pl.ds(0, half_snaps)])
+        queries = turn(queries)
+        scores = [masked(keys[at], queries[at], visible) for at in range(groups)]
+        for at, out in enumerate(attend([scores], [values], before)):
+            outgoing[at] = out.astype(jnp.bfloat16)
+        for peer in mirrored[:-1]:
+            hand_back(outgoing, 0, peer, all_rows, all_rows, 0)
+        load(outgoing.at[me_feat, me_snap % half_dev], returned.at[part, rank], 0)
+        settle(vertex_rows.at[pl.ds(0, half_snaps), lent_rows], spread_recv.at[1])
+        lent = vertex_rows[
+            pl.ds(half_snaps, half_snaps), pl.ds(vert_dev - 2 * SUBLANES, 2 * SUBLANES)
+        ].astype(jnp.float32)[:, SUBLANES:]
+        flat = lent.reshape(group_rows, width)
+        rounded = flat.astype(jnp.bfloat16)
+        turned = turn(project(rounded, 2))
+        scores = [masked(project(rounded, 3)[0], turned[0], visible)]
+        scores_low = [masked(keys[groups - 1], turned[0], same)]
+        outs = attend(
+            [scores_low, scores], [values[groups - 1 :], project(rounded, 4)], [flat]
+        )
+        for at, out in enumerate(outs):
+            lending[at] = out.astype(jnp.bfloat16)
+        for peer in mirrored:
+            hand_back(lending, 1, peer, lent_rows, pl.ds(0, SUBLANES), 1)
+        settle(hidden_two.at[:, kept_rows], spread_send.at[1])
+        settle(hidden_two.at[pl.ds(0, half_snaps - 1)], spread_send.at[0])
+        pltpu.make_async_copy(
+            outgoing.at[0, 0], returned.at[part, rank], load_sem.at[0]
+        ).wait()
+        everyone = outgoing.reshape(total, vert_dev, LANES).at[pl.ds(0, total - 1)]
+        settle(everyone, return_recv.at[0])
+        settle(everyone, return_send.at[0])
+        settle(lending, return_send.at[1])
 
     @pl.when(is_high)
     def _():
-        settle(vertex_rows.at[pl.ds(0, half_snaps)], spread_recv.at[0])
+        settle(vertex_rows.at[pl.ds(0, half_snaps - 1), kept_rows], spread_recv.at[1])
+        queries, keys, values, before = own_part(vertex_rows[pl.ds(half_snaps, half_snaps)])
+        queries = turn(queries[:-1])
+        scores = [masked(keys[at], queries[at], visible) for at in range(groups - 1)]
+        settle(vertex_rows.at[pl.ds(0, half_snaps), kept_rows], spread_recv.at[0])
         flat_low = vertex_rows[pl.ds(0, half_snaps)].reshape(half_snaps * vert_dev, width)
         keys_low, values_low = project(flat_low, 3), project(flat_low, 4)
         scores_low = [
-            [jnp.where(same, each, masked_score) for each in score(keys_low[at], queries[at])]
-            for at in range(groups)
+            masked(keys_low[at], queries[at], same) for at in range(groups - 1)
         ]
-        attend([scores_low, scores], [values_low, values])
-
-    total = half_dev * n_feat
-    me = (me_snap % half_dev) * n_feat + me_feat
-    for mask in (14, 15, 12, 13, 10, 11, 6, 7, 8, 9, 4, 5, 2, 3, 1):
-        peer = flip(me // 2, mask // 2) * 2 + (1 - me % 2 if mask % 2 else me % 2)
-        pltpu.make_async_remote_copy(
-            src_ref=outgoing.at[peer % n_feat, peer // n_feat],
-            dst_ref=returned.at[part, rank],
-            send_sem=return_send,
-            recv_sem=return_recv,
-            device_id=(half * half_dev + peer // n_feat, peer % n_feat),
-            device_id_type=MESH,
-        ).start()
-    own_copy = load(outgoing.at[me_feat, me_snap % half_dev], returned.at[part, rank], 0)
+        outs = attend([scores_low, scores], [values_low, values], before[:-1])
+        for at, out in enumerate(outs):
+            outgoing[at, :, kept_rows] = out.astype(jnp.bfloat16)
+        for peer in mirrored[:-1]:
+            hand_back(outgoing, 1, peer, kept_rows, kept_rows, 0)
+        own_copy = load(
+            outgoing.at[me_feat, me_snap % half_dev, kept_rows],
+            returned.at[part, rank, kept_rows],
+            0,
+        )
+        settle(hidden_two.at[:, lent_rows], spread_send.at[0])
+        settle(hidden_two.at[pl.ds(0, half_snaps - 1), kept_rows], spread_send.at[1])
+        own_copy.wait()
+        everyone = outgoing.reshape(total, vert_dev, LANES).at[pl.ds(0, total - 1), kept_rows]
+        settle(everyone, return_recv.at[0])
+        settle(lending, return_recv.at[1])
+        settle(everyone, return_send.at[0])
+
     settle(pieces.at[pl.ds(0, n_feat - 1)], gather_send)
-
-    @pl.when(is_low)
-    def _():
-        settle(hidden_two.at[pl.ds(0, half_snaps)], spread_send.at[1])
-        settle(hidden_two.at[pl.ds(0, half_snaps - 1)], spread_send.at[0])
-
-    @pl.when(is_high)
-    def _():
-        settle(hidden_two.at[pl.ds(0, half_snaps - 1)], spread_send.at[1])
-
-    own_copy.wait()
-    everyone = outgoing.reshape(total, vert_dev, LANES).at[pl.ds(0, total - 1)]
-    settle(everyone, return_recv)
-    settle(everyone, return_send)
 
 
 def on_device_fused(n_snap, n_feat, *operands):
@@ -570,6 +647,7 @@
         scratch_shapes=[
             pltpu.VMEM((slot_total, tile_side, tile_side), kept),
             pltpu.VMEM((6, width, width), kept),
+            pltpu.VMEM((feat_width, vert_count), kept),
             pltpu.VMEM((n_feat, feat_width, vert_count), kept),
             pltpu.VMEM((vert_count, vert_count), kept),
             pltpu.VMEM((vert_count, width), kept),
@@ -577,13 +655,14 @@
             pltpu.VMEM((half_snaps, vert_dev, width), kept),
             pltpu.VMEM((snaps, vert_dev, width), kept),
             pltpu.VMEM((n_feat, n_snap // 2, vert_dev, LANES), kept),
-            pltpu.SemaphoreType.DMA((6,)),
+            pltpu.VMEM((n_feat, n_snap // 2, SUBLANES, LANES), kept),
+            pltpu.SemaphoreType.DMA((7,)),
             pltpu.SemaphoreType.DMA,
             pltpu.SemaphoreType.DMA((CHUNKS + 1,)),
             pltpu.SemaphoreType.DMA((2,)),
             pltpu.SemaphoreType.DMA((2,)),
-            pltpu.SemaphoreType.DMA,
-            pltpu.SemaphoreType.DMA,
+            pltpu.SemaphoreType.DMA((2,)),
+            pltpu.SemaphoreType.DMA((2,)),
             pltpu.SemaphoreType.REGULAR((n_snap // 2,)),
             pltpu.SMEM((snap_dev, slot_total), jnp.int32),
             pltpu.SMEM((snap_dev, slot_total), jnp.int32),

time: 21 us -> 19.1 us (0.910)
  the two profiles are of different devices: /device:TPU:17 before, /device:TPU:0 now
where the time goes in v3:
time: 19.1 us; the launch traced here: 18.7 us
  Pallas kernels  17.9 us (94%)
  local copies, waits for them, and re-layouts  0.77 us (4%)
    pallas_call x1, Pallas kernels, on_device_fused(): pl.pallas_call(functools.partial(fused_kernel, n_snap, n_feat), out_shape...  17.9 us
    transpose x1, local copies, waits for them, and re-layouts, on_device_fused(): result = jnp.transpose(result.reshape(vert_count, LANES))  0.77 us

profile of v3, /device:TPU:0, one launch (start us, length us, event | category | flops | bytes accessed | tf_op | source)
XLA Modules:
  0.0 18.7 jit_solution(7922294180353176551)
XLA Ops:
  0.0 17.9 %shard_map.109 = bf16[2,8,32,128]{3,2,1,0:T(8,128)(2,1)S(1)} custom-call(s32[2,8]{1,0:T(2,128)} %rows_hbm.1, s32[2,8]{1,0:T(2,128)} %cols_hbm.1, s32[2]{0:T(128)} %counts_hbm.1, bf16[2,64,512]{2,1,0:T(8,128)(2,1)} %bitcast.8, bf16[2,8,128,128]{3,2,1,0:T(8,128)(2,1)} %tiles_ref.1, bf16[256,256]{1,0:T(8,128)(2,1)} %w_one.1, bf16[256,256]{1,0:T(8,128)(2,1)} %w_two.1, ...), custom_call_target="tpu_custom_call" | custom-call | tf_op jit(solution)/shard_map/pallas_call | solution.py:642
  17.9 0.8 %copy.12 = bf16[128,512]{1,0:T(8,128)(2,1)} copy(bf16[128,512]{0,1:T(8,128)(2,1)S(1)} %bitcast.7) | data formatting | bytes 262144 | tf_op jit(solution)/shard_map/transpose | solution.py:673

commit v4 on v3

--- a/solution.py
+++ b/solution.py
@@ -135,6 +135,7 @@
 
 LANES = 128
 CHUNKS = 2
+LENT = (1, 2)
 SUBLANES = 8
 MESH = pl.DeviceIdType.MESH
 
@@ -233,12 +234,17 @@
     leads = part == parts - 1
     lead_count = leads.astype(jnp.int32)
     tell_mates(barrier)
-    tell_column(barrier)
 
     @pl.when(leads)
     def _():
         signal(barrier, (twin, me_feat))
 
+    @pl.when(leads | (column_count == 1))
+    def _():
+        tell_column(barrier)
+
+    level = me_snap // plane
+    near_end = (level == 1).astype(jnp.int32) + (level == n_snap // plane - 2).astype(jnp.int32)
     partner = (me_feat + parts) % n_feat
     away_load = load(feat_ref.at[partner // parts], away, 6)
     own_load = load(feat_ref.at[local], pieces.at[me_feat], 0)
@@ -250,13 +256,13 @@
     ]
     tile_load = load(tiles_ref.at[local], tiles, 1)
     weight_list = (w_one, w_two, w_query, w_key, w_value, w_out)
-    pl.semaphore_wait(barrier, len(mates) + lead_count * (1 + parts * column_count))
+    pl.semaphore_wait(barrier, len(mates) + lead_count * (1 + column_count + near_end))
 
     mate = local * parts + 1 - part
     across = (partner // parts) * parts + 1 - part
-    chunk = feat_width // (2 * CHUNKS)
+    chunk = feat_width // CHUNKS
     spans = [pl.ds(at * chunk, chunk) for at in range(CHUNKS)]
-    rest = pl.ds(feat_width // 2, feat_width // 2)
+    whole = pl.ds(0, feat_width)
 
     def gather(source, span, at, peer):
         pltpu.make_async_remote_copy(
@@ -269,12 +275,19 @@
         ).start()
 
     away_load.wait()
-    for at in range(CHUNKS):
-        gather(away, spans[at], at, partner)
-    gather(away, rest, CHUNKS, partner)
-    gather(away, rest, CHUNKS, across)
+
+    @pl.when(leads)
+    def _():
+        for at in range(CHUNKS):
+            gather(away, spans[at], at, partner)
+
+    @pl.when(part == 0)
+    def _():
+        gather(away, whole, CHUNKS, partner)
+        gather(away, whole, CHUNKS, across)
+
     own_load.wait()
-    gather(pieces.at[me_feat], pl.ds(0, feat_width), CHUNKS, mate)
+    gather(pieces.at[me_feat], whole, CHUNKS, mate)
 
     def relay(at):
         passed = pieces.at[partner, spans[at]]
@@ -328,6 +341,7 @@
 
     strips = tile_side // strip
     lax.fori_loop(0, strips // 2, build, 0)
+    lax.fori_loop(strips // 2, strips, build, 0)
     for hop in range(hops - 1):
 
         @pl.when(leads)
@@ -335,24 +349,30 @@
             pl.semaphore_wait(heard.at[hop], column_count)
             tell_column(heard.at[hop + 1])
 
-    lax.fori_loop(strips // 2, strips, build, 0)
 
     @pl.when(leads)
     def _():
         pl.semaphore_wait(heard.at[hops - 1], column_count)
         signal(heard.at[hops], (twin, me_feat))
 
-    for at in range(CHUNKS):
-        relay(at)
-
     @pl.when(leads)
     def _():
+        for at in range(CHUNKS):
+            relay(at)
         pl.semaphore_wait(heard.at[hops], 1)
         tell_mates(heard.at[hops + 1])
 
 
     settle(weights, load_sem.at[5])
-    settle(pieces.at[:, pl.ds(0, 5 * feat_width // 8)], gather_recv.at[CHUNKS])
+
+    @pl.when(leads)
+    def _():
+        settle(pieces.at[pl.ds(0, n_feat - 2)], gather_recv.at[CHUNKS])
+
+    @pl.when(part == 0)
+    def _():
+        settle(pieces.at[pl.ds(0, n_feat - 1)], gather_recv.at[CHUNKS])
+
     features[...] = jnp.transpose(pieces[...].reshape(width, vert_count))
 
     def mix(lhs, source, before, weight):
@@ -365,8 +385,12 @@
     hidden_one[...] = mix(adjacency[...], features[...], features[...], weights[0])
     pl.semaphore_wait(heard.at[hops + 1], snap_dev - lead_count)
 
-    kept_rows = pl.ds(0, vert_dev - SUBLANES)
-    lent_rows = pl.ds(vert_dev - SUBLANES, SUBLANES)
+    side = half_snaps // 2
+    far = rank // side
+    keeps = [vert_dev - each * SUBLANES for each in LENT]
+    lends = [each * SUBLANES for each in LENT]
+    kept_rows = [pl.ds(0, each) for each in keeps]
+    lent_rows = [pl.ds(keep, lend) for keep, lend in zip(keeps, lends)]
     all_rows = pl.ds(0, vert_dev)
 
     def spread_to(target_half, peer, rows):
@@ -402,13 +426,23 @@
         spread_half(0, all_rows)
         for high in (1, 0):
             for mask in (3, 2, 1, 0):
-                spread_to(1, high * (half_snaps // 2) + flip(near, mask), kept_rows)
+                spread_to(1, high * side + flip(near, mask), kept_rows[high])
     @pl.when(is_high)
     def _():
         for high in (0, 1):
             for mask in (3, 2, 1, 0):
-                spread_to(0, high * (half_snaps // 2) + flip(near, mask), lent_rows)
-        spread_half(1, kept_rows)
+                spread_to(0, high * side + flip(near, mask), lent_rows[high])
+
+    for high in range(2):
+
+        @pl.when(is_high & (far == high))
+        def _():
+            for mask in (7, 6, 5, 3, 4, 2, 1):
+                peer_high = high if mask < 4 else 1 - high
+                spread_to(
+                    1, peer_high * side + flip(near, mask % 4), kept_rows[peer_high]
+                )
+
 
     vertex_rows[own] = hidden_two[rank]
 
@@ -538,6 +572,7 @@
         return outs
 
     total = half_dev * n_feat
+    outgoing_rows = outgoing.reshape(total * vert_dev, LANES)
     me = (me_snap % half_dev) * n_feat + me_feat
 
     def hand_back(source, target_half, peer, rows, source_rows, at):
@@ -570,61 +605,90 @@
         for peer in mirrored[:-1]:
             hand_back(outgoing, 0, peer, all_rows, all_rows, 0)
         load(outgoing.at[me_feat, me_snap % half_dev], returned.at[part, rank], 0)
-        settle(vertex_rows.at[pl.ds(0, half_snaps), lent_rows], spread_recv.at[1])
-        lent = vertex_rows[
-            pl.ds(half_snaps, half_snaps), pl.ds(vert_dev - 2 * SUBLANES, 2 * SUBLANES)
-        ].astype(jnp.float32)[:, SUBLANES:]
-        flat = lent.reshape(group_rows, width)
-        rounded = flat.astype(jnp.bfloat16)
-        turned = turn(project(rounded, 2))
-        scores = [masked(project(rounded, 3)[0], turned[0], visible)]
-        scores_low = [masked(keys[groups - 1], turned[0], same)]
-        outs = attend(
-            [scores_low, scores], [values[groups - 1 :], project(rounded, 4)], [flat]
-        )
-        for at, out in enumerate(outs):
-            lending[at] = out.astype(jnp.bfloat16)
-        for peer in mirrored:
-            hand_back(lending, 1, peer, lent_rows, pl.ds(0, SUBLANES), 1)
-        settle(hidden_two.at[:, kept_rows], spread_send.at[1])
+        for high in range(2):
+
+            @pl.when(far == high)
+            def _():
+                count = LENT[high]
+                settle(
+                    vertex_rows.at[pl.ds(0, half_snaps), lent_rows[high]], spread_recv.at[1]
+                )
+                base = keeps[high] // (2 * SUBLANES) * 2 * SUBLANES
+                lent = vertex_rows[
+                    pl.ds(half_snaps, half_snaps), pl.ds(base, vert_dev - base)
+                ].astype(jnp.float32)[:, keeps[high] - base :]
+                flats = split(lent)
+                rounded = jnp.concatenate(flats, axis=0).astype(jnp.bfloat16)
+
+                def lent_part(at):
+                    out = jnp.dot(rounded, weights[at], preferred_element_type=jnp.float32)
+                    return [
+                        out[each * group_rows : (each + 1) * group_rows]
+                        for each in range(count)
+                    ]
+
+                turned = turn(lent_part(2))
+                lent_keys = lent_part(3)
+                scores = [masked(lent_keys[at], turned[at], visible) for at in range(count)]
+                scores_low = [
+                    masked(keys[groups - count + at], turned[at], same)
+                    for at in range(count)
+                ]
+                outs = attend(
+                    [scores_low, scores], [values[groups - count :], lent_part(4)], flats
+                )
+                for at, out in enumerate(outs):
+                    lending[at, :, pl.ds(0, lends[high])] = out.astype(jnp.bfloat16)
+                for peer in mirrored:
+                    hand_back(lending, 1, peer, lent_rows[high], pl.ds(0, lends[high]), 1)
+                settle(outgoing_rows.at[pl.ds(0, total * lends[high])], return_send.at[1])
+
+        settle(hidden_one.at[pl.ds(0, side * sum(keeps))], spread_send.at[1])
         settle(hidden_two.at[pl.ds(0, half_snaps - 1)], spread_send.at[0])
         pltpu.make_async_copy(
             outgoing.at[0, 0], returned.at[part, rank], load_sem.at[0]
         ).wait()
-        everyone = outgoing.reshape(total, vert_dev, LANES).at[pl.ds(0, total - 1)]
+        everyone = outgoing_rows.at[pl.ds(0, (total - 1) * vert_dev)]
         settle(everyone, return_recv.at[0])
         settle(everyone, return_send.at[0])
-        settle(lending, return_send.at[1])
-
-    @pl.when(is_high)
-    def _():
-        settle(vertex_rows.at[pl.ds(0, half_snaps - 1), kept_rows], spread_recv.at[1])
-        queries, keys, values, before = own_part(vertex_rows[pl.ds(half_snaps, half_snaps)])
-        queries = turn(queries[:-1])
-        scores = [masked(keys[at], queries[at], visible) for at in range(groups - 1)]
-        settle(vertex_rows.at[pl.ds(0, half_snaps), kept_rows], spread_recv.at[0])
-        flat_low = vertex_rows[pl.ds(0, half_snaps)].reshape(half_snaps * vert_dev, width)
-        keys_low, values_low = project(flat_low, 3), project(flat_low, 4)
-        scores_low = [
-            masked(keys_low[at], queries[at], same) for at in range(groups - 1)
-        ]
-        outs = attend([scores_low, scores], [values_low, values], before[:-1])
-        for at, out in enumerate(outs):
-            outgoing[at, :, kept_rows] = out.astype(jnp.bfloat16)
-        for peer in mirrored[:-1]:
-            hand_back(outgoing, 1, peer, kept_rows, kept_rows, 0)
-        own_copy = load(
-            outgoing.at[me_feat, me_snap % half_dev, kept_rows],
-            returned.at[part, rank, kept_rows],
-            0,
-        )
-        settle(hidden_two.at[:, lent_rows], spread_send.at[0])
-        settle(hidden_two.at[pl.ds(0, half_snaps - 1), kept_rows], spread_send.at[1])
-        own_copy.wait()
-        everyone = outgoing.reshape(total, vert_dev, LANES).at[pl.ds(0, total - 1), kept_rows]
-        settle(everyone, return_recv.at[0])
-        settle(lending, return_recv.at[1])
-        settle(everyone, return_send.at[0])
+
+    for high in range(2):
+
+        @pl.when(is_high & (far == high))
+        def _():
+            keep = keeps[high]
+            count = groups - LENT[high]
+            kept = kept_rows[high]
+            settle(vertex_rows.at[pl.ds(0, half_snaps - 1), kept], spread_recv.at[1])
+            queries, keys, values, before = own_part(
+                vertex_rows[pl.ds(half_snaps, half_snaps)]
+            )
+            queries = turn(queries[:count])
+            scores = [masked(keys[at], queries[at], visible) for at in range(count)]
+            settle(vertex_rows.at[pl.ds(0, half_snaps), kept], spread_recv.at[0])
+            flat_low = vertex_rows[pl.ds(0, half_snaps)].reshape(half_snaps * vert_dev, width)
+            keys_low, values_low = project(flat_low, 3), project(flat_low, 4)
+            scores_low = [masked(keys_low[at], queries[at], same) for at in range(count)]
+            outs = attend([scores_low, scores], [values_low, values], before[:count])
+            for at, out in enumerate(outs):
+                outgoing[at, :, kept] = out.astype(jnp.bfloat16)
+            for peer in mirrored[:-1]:
+                hand_back(outgoing, 1, peer, kept, kept, 0)
+            own_copy = load(
+                outgoing.at[me_feat, me_snap % half_dev, kept], returned.at[part, rank, kept], 0
+            )
+            settle(hidden_one.at[pl.ds(0, side * sum(lends))], spread_send.at[0])
+            settle(
+                hidden_one.at[pl.ds(0, side * sum(keeps) - keep)], spread_send.at[1]
+            )
+            own_copy.wait()
+            settle(
+                outgoing_rows.at[pl.ds(0, total // 2 * sum(keeps) - keep)], return_recv.at[0]
+            )
+            settle(
+                outgoing_rows.at[pl.ds(0, total // 2 * sum(lends))], return_recv.at[1]
+            )
+            settle(outgoing_rows.at[pl.ds(0, (total - 1) * keep)], return_send.at[0])
 
     settle(pieces.at[pl.ds(0, n_feat - 1)], gather_send)
 
@@ -655,7 +719,7 @@
             pltpu.VMEM((half_snaps, vert_dev, width), kept),
             pltpu.VMEM((snaps, vert_dev, width), kept),
             pltpu.VMEM((n_feat, n_snap // 2, vert_dev, LANES), kept),
-            pltpu.VMEM((n_feat, n_snap // 2, SUBLANES, LANES), kept),
+            pltpu.VMEM((n_feat, n_snap // 2, max(LENT) * SUBLANES, LANES), kept),
             pltpu.SemaphoreType.DMA((7,)),
             pltpu.SemaphoreType.DMA,
             pltpu.SemaphoreType.DMA((CHUNKS + 1,)),
@@ -686,6 +750,7 @@
         and n_snap % 4 == 0
         and vert_count % (n_feat // snap_dev * snaps * SUBLANES) == 0
         and snaps * SUBLANES == LANES
+        and vert_count >= 4 * SUBLANES * snaps
         and slot_total <= 16
         and vert_count <= 1024
     )

time: 19.1 us -> 18.3 us (0.958); the launches traced: 18.7 us -> 18.2 us
  Pallas kernels: 17.9 us -> 17.4 us
    pallas_call x1, Pallas kernels: 17.9 us -> 17.4 us  [on_device_fused(): pl.pallas_call(functools.partial(fused_kernel, n_snap, n_feat), out_shape...]
where the time goes in v4:
time: 18.3 us; the launch traced here: 18.2 us
  Pallas kernels  17.4 us (95%)
  local copies, waits for them, and re-layouts  0.77 us (4%)
    pallas_call x1, Pallas kernels, on_device_fused(): pl.pallas_call(functools.partial(fused_kernel, n_snap, n_feat), out_shape...  17.4 us
    transpose x1, local copies, waits for them, and re-layouts, on_device_fused(): result = jnp.transpose(result.reshape(vert_count, LANES))  0.77 us

profile of v4, /device:TPU:0, one launch (start us, length us, event | category | flops | bytes accessed | tf_op | source)
XLA Modules:
  0.0 18.2 jit_solution(854359812411768099)
XLA Ops:
  0.0 17.4 %shard_map.109 = bf16[2,8,32,128]{3,2,1,0:T(8,128)(2,1)S(1)} custom-call(s32[2,8]{1,0:T(2,128)} %rows_hbm.1, s32[2,8]{1,0:T(2,128)} %cols_hbm.1, s32[2]{0:T(128)} %counts_hbm.1, bf16[2,64,512]{2,1,0:T(8,128)(2,1)} %bitcast.8, bf16[2,8,128,128]{3,2,1,0:T(8,128)(2,1)} %tiles_ref.1, bf16[256,256]{1,0:T(8,128)(2,1)} %w_one.1, bf16[256,256]{1,0:T(8,128)(2,1)} %w_two.1, ...), custom_call_target="tpu_custom_call" | custom-call | tf_op jit(solution)/shard_map/pallas_call | solution.py:706
  17.4 0.8 %copy.12 = bf16[128,512]{1,0:T(8,128)(2,1)} copy(bf16[128,512]{0,1:T(8,128)(2,1)S(1)} %bitcast.7) | data formatting | bytes 262144 | tf_op jit(solution)/shard_map/transpose | solution.py:737

commit v5 on v4

--- a/solution.py
+++ b/solution.py
@@ -274,6 +274,8 @@
             device_id_type=MESH,
         ).start()
 
+    own_load.wait()
+    gather(pieces.at[me_feat], whole, CHUNKS, mate)
     away_load.wait()
 
     @pl.when(leads)
@@ -286,8 +288,6 @@
         gather(away, whole, CHUNKS, partner)
         gather(away, whole, CHUNKS, across)
 
-    own_load.wait()
-    gather(pieces.at[me_feat], whole, CHUNKS, mate)
 
     def relay(at):
         passed = pieces.at[partner, spans[at]]
@@ -373,17 +373,17 @@
     def _():
         settle(pieces.at[pl.ds(0, n_feat - 1)], gather_recv.at[CHUNKS])
 
-    features[...] = jnp.transpose(pieces[...].reshape(width, vert_count))
-
-    def mix(lhs, source, before, weight):
-        spread = jnp.dot(lhs, source, preferred_element_type=jnp.float32)
+    def mix(lhs, source, before, weight, turned=None):
+        if turned is None:
+            spread = jnp.dot(lhs, source, preferred_element_type=jnp.float32)
+        else:
+            spread = lax.dot_general(
+                lhs, turned, (((1,), (1,)), ((), ())), preferred_element_type=jnp.float32
+            )
         mixed = jnp.dot(
             spread.astype(jnp.bfloat16), weight, preferred_element_type=jnp.float32
         )
         return (before.astype(jnp.float32) + jnp.maximum(mixed, 0.0)).astype(jnp.bfloat16)
-
-    hidden_one[...] = mix(adjacency[...], features[...], features[...], weights[0])
-    pl.semaphore_wait(heard.at[hops + 1], snap_dev - lead_count)
 
     side = half_snaps // 2
     far = rank // side
@@ -417,9 +417,27 @@
 
     near = rank % (half_snaps // 2)
     own_rows = pl.ds(pl.multiple_of(part * part_rows, part_rows), part_rows)
-    hidden_two[...] = mix(
-        adjacency[own_rows, :], hidden_one[...], hidden_one[own_rows, :], weights[1]
-    ).reshape(half_snaps, vert_dev, width)
+    turned = pieces[...].reshape(width, vert_count)
+    block = vert_count // 1
+    spread_two = jnp.zeros((part_rows, width), jnp.float32)
+    for first in range(0, vert_count, block):
+        before = jnp.transpose(turned[:, first : first + block])
+        hidden = mix(adjacency[first : first + block, :], None, before, weights[0], turned)
+        hidden_one[first : first + block, :] = hidden
+        spread_two += jnp.dot(
+            adjacency[own_rows, first : first + block],
+            hidden,
+            preferred_element_type=jnp.float32,
+        )
+    mixed_two = jnp.dot(
+        spread_two.astype(jnp.bfloat16), weights[1], preferred_element_type=jnp.float32
+    )
+    hidden_two[...] = (
+        (hidden_one[own_rows, :].astype(jnp.float32) + jnp.maximum(mixed_two, 0.0))
+        .astype(jnp.bfloat16)
+        .reshape(half_snaps, vert_dev, width)
+    )
+    pl.semaphore_wait(heard.at[hops + 1], snap_dev - lead_count)
 
     @pl.when(is_low)
     def _():

time: 18.3 us -> 18.1 us (0.989)
  Pallas kernels: 17.4 us -> 17.2 us
    pallas_call x1, Pallas kernels: 17.4 us -> 17.2 us  [on_device_fused(): pl.pallas_call(functools.partial(fused_kernel, n_snap, n_feat), out_shape...]
where the time goes in v5:
time: 18.1 us; the launch traced here: 18 us
  Pallas kernels  17.2 us (95%)
  local copies, waits for them, and re-layouts  0.77 us (4%)
    pallas_call x1, Pallas kernels, on_device_fused(): pl.pallas_call(functools.partial(fused_kernel, n_snap, n_feat), out_shape...  17.2 us
    transpose x1, local copies, waits for them, and re-layouts, on_device_fused(): result = jnp.transpose(result.reshape(vert_count, LANES))  0.77 us

profile of v5, /device:TPU:0, one launch (start us, length us, event | category | flops | bytes accessed | tf_op | source)
XLA Modules:
  0.0 18.0 jit_solution(3589782875901002459)
XLA Ops:
  0.0 17.2 %shard_map.109 = bf16[2,8,32,128]{3,2,1,0:T(8,128)(2,1)S(1)} custom-call(s32[2,8]{1,0:T(2,128)} %rows_hbm.1, s32[2,8]{1,0:T(2,128)} %cols_hbm.1, s32[2]{0:T(128)} %counts_hbm.1, bf16[2,64,512]{2,1,0:T(8,128)(2,1)} %bitcast.8, bf16[2,8,128,128]{3,2,1,0:T(8,128)(2,1)} %tiles_ref.1, bf16[256,256]{1,0:T(8,128)(2,1)} %w_one.1, bf16[256,256]{1,0:T(8,128)(2,1)} %w_two.1, ...), custom_call_target="tpu_custom_call" | custom-call | tf_op jit(solution)/shard_map/pallas_call | solution.py:724
  17.2 0.8 %copy.12 = bf16[128,512]{1,0:T(8,128)(2,1)} copy(bf16[128,512]{0,1:T(8,128)(2,1)S(1)} %bitcast.7) | data formatting | bytes 262144 | tf_op jit(solution)/shard_map/transpose | solution.py:755

commit v6 on v5

--- a/solution.py
+++ b/solution.py
@@ -412,7 +412,7 @@
         return flipped
 
     def spread_half(target_half, rows):
-        for mask in (7, 6, 5, 3, 4, 2, 1):
+        for mask in (7, 3, 6, 5, 2, 1, 4):
             spread_to(target_half, flip(rank, mask), rows)
 
     near = rank % (half_snaps // 2)

time: 18.1 us -> 18.1 us (level)
  no operation moved by 1% of the time
where the time goes in v6:
time: 18.1 us; the launch traced here: 18 us
  Pallas kernels  17.2 us (95%)
  local copies, waits for them, and re-layouts  0.77 us (4%)
    pallas_call x1, Pallas kernels, on_device_fused(): pl.pallas_call(functools.partial(fused_kernel, n_snap, n_feat), out_shape...  17.2 us
    transpose x1, local copies, waits for them, and re-layouts, on_device_fused(): result = jnp.transpose(result.reshape(vert_count, LANES))  0.77 us

profile of v6, /device:TPU:0, one launch (start us, length us, event | category | flops | bytes accessed | tf_op | source)
XLA Modules:
  0.0 18.0 jit_solution(12746446422354707858)
XLA Ops:
  0.0 17.2 %shard_map.109 = bf16[2,8,32,128]{3,2,1,0:T(8,128)(2,1)S(1)} custom-call(s32[2,8]{1,0:T(2,128)} %rows_hbm.1, s32[2,8]{1,0:T(2,128)} %cols_hbm.1, s32[2]{0:T(128)} %counts_hbm.1, bf16[2,64,512]{2,1,0:T(8,128)(2,1)} %bitcast.8, bf16[2,8,128,128]{3,2,1,0:T(8,128)(2,1)} %tiles_ref.1, bf16[256,256]{1,0:T(8,128)(2,1)} %w_one.1, bf16[256,256]{1,0:T(8,128)(2,1)} %w_two.1, ...), custom_call_target="tpu_custom_call" | custom-call | tf_op jit(solution)/shard_map/pallas_call | solution.py:724
  17.2 0.8 %copy.12 = bf16[128,512]{1,0:T(8,128)(2,1)} copy(bf16[128,512]{0,1:T(8,128)(2,1)S(1)} %bitcast.7) | data formatting | bytes 262144 | tf_op jit(solution)/shard_map/transpose | solution.py:755
